TPU v7x, 512 devices: a whole 4x4x16 slice. The times are simulated.
512 devices in a mesh: req: 64 (over x, z), head: 8 (over y, core).
Axes of the slice: x: 4, y: 4, z: 16, core: 2. Of those that a mesh axis runs over, the one named last changes fastest.
Arguments:
- tokens: bfloat16 [320, 1024], P('req'), may hold values from -6 to 6
- norm_gain: float32 [1024], replicated, may hold values from 0.1 to 1.9
- w_qkv: bfloat16 [1024, 8, 384], P(None, 'head'), may hold values from -0.1875 to 0.1875
- persist_kv: bfloat16 [8, 16, 256], P('head'), may hold values from -9 to 9
- memory: bfloat16 [64, 8, 128, 128], P('req', 'head'), may hold values from -0.5 to 0.5
- cache_kv: bfloat16 [512, 512, 8, 256], P('req', None, 'head')
- piece_owner: int32 [512], P('req'), may hold values from 0 to 63, as said below
- piece_len: int32 [512], P('req'), may hold values from 1 to 512, as said below
- w_out: bfloat16 [8, 128, 1024], P('head'), may hold values from -0.1875 to 0.1875
Outputs:
- layer_out: bfloat16 [320, 1024], P('req', 'head')
Inputs may be any that keep to these rules, and one draw needn't show every extreme that they name: `piece_owner`: every request owns 1 to 16 pieces, and one request owns exactly 16. `piece_len`: some piece is full.
All inputs are finite; a program needn't handle non-finite values.
Results may differ from a plain program's by a relative error of at most 0.009.
The roundings to bfloat16 on the way count: a program that leaves them out, or rounds other values in their place, can miss the bound.
Values may be sent and summed in bfloat16 or wider, within the bound.
No kernel may reach another device: no remote copies, remote signals or barrier semaphores. Data moves between devices by JAX's collectives and lax.ppermute only.
A program may use at most 64 MiB of HBM per device.

v0:
```python
import jax
import jax.numpy as jnp
from jax import lax
from jax.sharding import PartitionSpec as P

DH = 128
NP = 16
Q = 5
PIECE = 512


masked_score = -1e30
norm_eps = 1e-06


def merged(shard, axis, combine):
    everything = jax.tree.map(lambda part: lax.all_gather(part, axis), shard)
    leading = jax.tree.map(lambda part: part[0], everything)

    def step(k, so_far):
        return combine(so_far, jax.tree.map(lambda part: part[k], everything))

    return lax.fori_loop(1, lax.axis_size(axis), step, leading)


def join_parts(first, second):
    peak = jnp.maximum(first[0], second[0])
    scale_one = jnp.exp(first[0] - peak)
    scale_two = jnp.exp(second[0] - peak)
    total = first[1] * scale_one + second[1] * scale_two
    summed = first[2] * scale_one[..., None] + second[2] * scale_two[..., None]
    return (peak, total, summed)


def dense_parts(peaks, totals, summed, piece_owner, total_reqs):
    f32 = jnp.float32
    onehot = piece_owner[:, None] == jnp.arange(total_reqs, dtype=jnp.int32)[None, :]
    peak_dev = jnp.max(jnp.where(onehot[:, :, None, None], peaks[:, None], masked_score), axis=0)
    factor = jnp.exp(peaks - peak_dev[piece_owner])
    onehot_f = onehot.astype(f32)
    total_dev = jnp.einsum(
        "sr,shq->rhq", onehot_f, totals * factor, precision=lax.Precision.HIGHEST
    )
    summed_dev = jnp.einsum(
        "sr,shqe->rhqe", onehot_f, summed * factor[..., None], precision=lax.Precision.HIGHEST
    )
    return (peak_dev, total_dev, summed_dev)


def shards(tokens, norm_gain, w_qkv, persist_kv, memory, cache_kv, piece_owner, piece_len, w_out):
    f32 = jnp.float32
    rows = tokens.shape[0]
    heads = w_qkv.shape[1]
    req_dev = memory.shape[0]
    xf = tokens.astype(f32)
    normed = (
        xf * lax.rsqrt(jnp.mean(xf * xf, axis=-1, keepdims=True) + norm_eps) * norm_gain
    ).astype(jnp.bfloat16)
    proj = jnp.einsum("td,dhe->the", normed, w_qkv, preferred_element_type=f32)
    query = (proj[..., :DH] * DH ** (-0.5)).astype(jnp.bfloat16)
    new_key = proj[..., DH : 2 * DH].astype(jnp.bfloat16)
    new_value = proj[..., 2 * DH :].astype(jnp.bfloat16)
    all_query = lax.all_gather(query, "req", axis=0, tiled=True)
    query_all4 = all_query.reshape(-1, Q, heads, DH)
    total_reqs = query_all4.shape[0]
    query_rows = query_all4[piece_owner]
    scores = jnp.einsum(
        "sqhe,skhe->shqk", query_rows, cache_kv[..., :DH], preferred_element_type=f32
    )
    valid = (jnp.arange(PIECE)[None, :] < piece_len[:, None])[:, None, None, :]
    scores = jnp.where(valid, scores, masked_score)
    peaks = jnp.max(scores, axis=-1)
    weight = jnp.where(valid, jnp.exp(scores - peaks[..., None]), 0.0)
    totals = jnp.sum(weight, axis=-1)
    summed = jnp.einsum(
        "shqk,skhe->shqe",
        weight.astype(jnp.bfloat16),
        cache_kv[..., DH:],
        preferred_element_type=f32,
    )
    peak_dev, total_dev, summed_dev = dense_parts(peaks, totals, summed, piece_owner, total_reqs)
    peak_all, total_all, summed_all = merged((peak_dev, total_dev, summed_dev), "req", join_parts)
    start = lax.axis_index("req") * req_dev
    peak_cache = lax.dynamic_slice_in_dim(peak_all, start, req_dev, 0)
    total_cache = lax.dynamic_slice_in_dim(total_all, start, req_dev, 0)
    summed_cache = lax.dynamic_slice_in_dim(summed_all, start, req_dev, 0)
    query4 = query.reshape(req_dev, Q, heads, DH)
    key4 = new_key.reshape(req_dev, Q, heads, DH)
    value4 = new_value.reshape(req_dev, Q, heads, DH)
    score_persist = jnp.einsum(
        "rqhe,hne->rhqn", query4, persist_kv[..., :DH], preferred_element_type=f32
    )
    score_new = jnp.einsum("rqhe,rkhe->rhqk", query4, key4, preferred_element_type=f32)
    causal = jnp.arange(Q)[:, None] >= jnp.arange(Q)[None, :]
    score_new = jnp.where(causal, score_new, masked_score)
    score_own = jnp.concatenate([score_persist, score_new], axis=-1)
    peak_own = jnp.max(score_own, axis=-1)
    weight_own = jnp.exp(score_own - peak_own[..., None])
    total_own = jnp.sum(weight_own, axis=-1)
    rounded_own = weight_own.astype(jnp.bfloat16)
    summed_own = jnp.einsum(
        "rhqn,hne->rhqe", rounded_own[..., :NP], persist_kv[..., DH:], preferred_element_type=f32
    )
    summed_own = summed_own + jnp.einsum(
        "rhqk,rkhe->rhqe", rounded_own[..., NP:], value4, preferred_element_type=f32
    )
    peak_total = jnp.maximum(peak_cache, peak_own)
    scale_cache = jnp.exp(peak_cache - peak_total)
    scale_own = jnp.exp(peak_own - peak_total)
    total_final = total_cache * scale_cache + total_own * scale_own
    summed_final = summed_cache * scale_cache[..., None] + summed_own * scale_own[..., None]
    attended = summed_final / total_final[..., None]
    recalled = jnp.einsum("rqhe,rhef->rhqf", query4, memory, preferred_element_type=f32)
    head_out = (attended + recalled).astype(jnp.bfloat16)
    head_out = jnp.transpose(head_out, (0, 2, 1, 3)).reshape(rows, heads, DH)
    partial_out = jnp.einsum("thd,hdf->tf", head_out, w_out, preferred_element_type=f32)
    return lax.psum_scatter(partial_out, "head", scatter_dimension=1, tiled=True).astype(
        jnp.bfloat16
    )


def solution(mesh):
    in_specs = (
        P("req", None),
        P(),
        P(None, "head", None),
        P("head", None, None),
        P("req", "head", None, None),
        P("req", None, "head", None),
        P("req"),
        P("req"),
        P("head", None, None),
    )
    out_specs = P("req", "head")
    return jax.shard_map(shards, mesh=mesh, in_specs=in_specs, out_specs=out_specs, check_vma=False)
```

profile of v0, /device:TPU:1, one launch (start us, length us, event | category | flops | bytes accessed | tf_op | source)
XLA Modules:
  0.0 403.2 jit_solution(6034953627705232493)
XLA Ops:
  9.0 0.9 fusion.60
  10.0 70.0 %all_gather.21 = bf16[320,1,128]{2,1,0:T(2,128)(2,1)S(1)} all-gather(bf16[5,1,128]{2,1,0:T(2,128)(2,1)S(1)} %copy.57), channel_id=1, replica_groups=mesh['req'=64,'head'=8] {'req'}, dimensions={0}, use_global_device_ids=true | all-gather | bytes 83200 | tf_op jit(solution)/shard_map/all_gather | solution.py:63
  81.9 1.7 fusion.61
  84.7 1.0 fusion.25
  85.8 63.4 %all-gather.3 = f32[64,64,5]{1,2,0:T(8,128)S(1)} all-gather(f32[1,64,5]{1,2,0:T(8,128)S(1)} %bitcast.171), channel_id=2, replica_groups=mesh['req'=64,'head'=8] {'req'}, dimensions={0}, use_global_device_ids=true | all-gather | bytes 83200 | tf_op jit(solution)/shard_map/all_gather | solution.py:17
  149.6 69.1 %all-gather.4 = f32[64,64,5]{1,2,0:T(8,128)S(1)} all-gather(f32[1,64,5]{1,2,0:T(8,128)S(1)} %convolution_bitcast_fusion.1), channel_id=3, replica_groups=mesh['req'=64,'head'=8] {'req'}, dimensions={0}, use_global_device_ids=true | all-gather | bytes 83200 | tf_op jit(solution)/shard_map/all_gather | solution.py:17
  219.5 39.2 %all-gather.7.cloned.1.call-done = f32[4096,5,128]{2,0,1:T(8,128)} async-done(((f32[64,5,128]{2,0,1:T(8,128)}), f32[4096,5,128]{2,0,1:T(8,128)}) %all-gather.7.cloned.1.call-update) | async-done | bytes 10485776 | tf_op jit(solution)/shard_map/all_gather | solution.py:17
  259.8 93.1 %while.19 = (s32[]{:T(128)}, f32[64,1,5]{0,1,2:T(1,128)S(1)}, f32[64,1,5]{0,1,2:T(1,128)S(1)}, f32[64,1,5,128]{3,2,1,0:T(8,128)S(1)}, f32[64,64,1,5]{1,2,3,0:T(1...) while((s32[]{:T(128)}, f32[64,1,5]{0,1,2:T(1,128)S(1)}, ...), condition=%wide.region_5.6_spmd, body=%wide.region_4.5_spmd.sunk | while | flops 124805 | bytes 837271 | solution.py:23
  259.9 0.9 constant_dynamic-slice_fusion.4
  261.3 0.9 constant_dynamic-slice_fusion.4
  262.8 0.9 constant_dynamic-slice_fusion.4
  264.3 0.9 constant_dynamic-slice_fusion.4
  265.8 0.9 constant_dynamic-slice_fusion.4
  267.3 0.9 constant_dynamic-slice_fusion.4
  268.7 0.9 constant_dynamic-slice_fusion.4
  270.2 0.9 constant_dynamic-slice_fusion.4
  271.7 0.9 constant_dynamic-slice_fusion.4
  273.2 0.9 constant_dynamic-slice_fusion.4
  274.6 0.9 constant_dynamic-slice_fusion.4
  288.0 0.9 constant_dynamic-slice_fusion.4
  316.0 0.9 constant_dynamic-slice_fusion.4
  344.1 0.9 constant_dynamic-slice_fusion.4
  354.6 40.5 %reduce-scatter.2.cloned.1.call-done = f32[5,128]{1,0:T(8,128)} async-done(((f32[5,1024]{1,0:T(8,128)}), f32[5,128]{1,0:T(8,128)}) %reduce-scatter.2.cloned.1.call-update) | async-done | bytes 2576 | tf_op jit(solution)/shard_map/reduce_scatter | solution.py:117
  395.1 1.2 convert_element_type.39
  (354 shorter events, 87.4 us)
Async XLA Ops:
  6.5 2.5 copy-start
  6.5 78.2 %copy-start.5 = (s32[8]{0:T(128)S(1)}, s32[8]{0:T(128)}, u32[]{:S(2)}) copy-start(s32[8]{0:T(128)} %param.17) | copy-start | bytes 100
  6.5 77.9 %copy-start.1 = (bf16[8,512,1,256]{3,1,2,0:T(8,128)(2,1)S(1)}, bf16[8,512,1,256]{3,1,2,0:T(8,128)(2,1)}, u32[]{:S(2)}) copy-start(bf16[8,512,1,256]{3,1,2,0:T(8,128)(2,1)} %param.16) | copy-start | bytes 6291460
  6.5 252.2 %all-gather.7.cloned.1.call-start = ((), (), s32[]{:S(2)}) async-start(), calls=%async_computation.2 | async-start | bytes 10649600 | tf_op jit(solution)/shard_map/all_gather | solution.py:17
  81.9 137.4 %copy-start.4 = (bf16[1,16,256]{2,1,0:T(8,128)(2,1)S(1)}, bf16[1,16,256]{2,1,0:T(8,128)(2,1)}, u32[]{:S(2)}) copy-start(bf16[1,16,256]{2,1,0:T(8,128)(2,1)} %param.14) | copy-start | bytes 24580
  85.8 309.3 %reduce-scatter.2.cloned.1.call-start = ((), (), s32[]{:S(2)}) async-start(), calls=%async_computation.1 | async-start | bytes 36864 | tf_op jit(solution)/shard_map/reduce_scatter | solution.py:117
  259.8 93.9 %copy-start.2 = (bf16[1,128,1024]{2,1,0:T(8,128)(2,1)S(1)}, bf16[1,128,1024]{2,1,0:T(8,128)(2,1)}, u32[]{:S(2)}) copy-start(bf16[1,128,1024]{2,1,0:T(8,128)(2,1)} %param.19) | copy-start | bytes 786436
  259.8 93.9 %copy-start.3 = (bf16[1,1,128,128]{3,2,1,0:T(8,128)(2,1)S(1)}, bf16[1,1,128,128]{3,2,1,0:T(8,128)(2,1)}, u32[]{:S(2)}) copy-start(bf16[1,1,128,128]{3,2,1,0:T(8,128)(2,1)} %param.15) | copy-start | bytes 98308
Sparse Core Ops, SparseCore 0:
  85.9 172.7 all-gather.6
  354.7 40.3 reduce-scatter.1
where the time goes:
time: 406 us; the launch traced here: 403 us
  blocking collectives  202 us (50%)
  waiting for transfers between devices  79.8 us (20%)
  local copies, waits for them, and re-layouts  74.2 us (18%)
  other arithmetic  25.4 us (6%)
  between operations  13.6 us (3%)
  matrix products  5.77 us (1%)
    all_gather x2, blocking collectives, merged(): everything = jax.tree.map(lambda part: lax.all_gather(part, axis), shard)  132 us
    all_gather x1, blocking collectives, shards(): all_query = lax.all_gather(query, 'req', axis=0, tiled=True)  70 us
    dynamic_slice x63, local copies, waits for them, and re-layouts, step(): return combine(so_far, jax.tree.map(lambda part: part[k], everything))  59.1 us
    reduce_scatter x1, waiting for transfers between devices, shards(): lax.psum_scatter(partial_out, 'head', scatter_dimension=1, tiled=True)  40.5 us
    all_gather x1, waiting for transfers between devices, merged(): everything = jax.tree.map(lambda part: lax.all_gather(part, axis), shard)  39.2 us
    add x63, other arithmetic, join_parts(): summed = first[2] * scale_one[..., None] + second[2] * scale_two[..., None]  17.9 us
    mul x126, local copies, waits for them, and re-layouts, join_parts(): summed = first[2] * scale_one[..., None] + second[2] * scale_two[..., None]  12.1 us
  transfers between devices with their start and end apart: 2, of which 2 were waited for; matrix products, arithmetic and copies ran while one was open for 0% of the time, Pallas kernels for 0%

commit v1 on v0

v1 whole, which is shorter than its diff:
```python
import jax
import jax.numpy as jnp
from jax import lax
from jax.experimental import pallas as pl
from jax.experimental.pallas import tpu as pltpu
from jax.sharding import PartitionSpec as P

DH = 128
NP = 16
Q = 5
ROWS = 8
M_ROW = 5
L_ROW = 6

masked_score = -1e30
norm_eps = 1e-06
f32 = jnp.float32
bf16 = jnp.bfloat16


def iota(shape, axis):
    return lax.broadcasted_iota(jnp.int32, shape, axis)


def dot(a, b):
    return jnp.dot(a, b, preferred_element_type=f32)


def dot_t(a, b):
    return lax.dot_general(a, b, (((1,), (1,)), ((), ())), preferred_element_type=f32)


def to_row(col, eye):
    return jnp.sum(jnp.where(eye, col, 0.0), axis=0, keepdims=True)


def to_col(row, eye):
    return jnp.sum(jnp.where(eye, jnp.broadcast_to(row, eye.shape), 0.0), axis=1, keepdims=True)


def packed(peak, total, summed, eye, row):
    tail = jnp.where(row == M_ROW, to_row(peak, eye), to_row(total, eye))
    return jnp.where(row < Q, summed, tail)


def project(tokens, gain, w_qkv, query_all, query, new_kv, padded):
    xf = tokens[...].astype(f32)
    inverse = lax.rsqrt(jnp.mean(xf * xf, axis=-1, keepdims=True) + norm_eps)
    normed = (xf * inverse * gain[...]).astype(bf16)
    padded[...] = jnp.zeros_like(padded)
    padded[0:Q, :] = dot(normed, w_qkv[...])
    proj = padded[...]
    q = (proj[:, :DH] * DH ** (-0.5)).astype(bf16)
    query[...] = q
    query_all[...] = jnp.broadcast_to(q[None], query_all.shape)
    new_kv[...] = proj[:, DH:].astype(bf16)


def attend(owner, length, query_all, query, new_kv, persist_kv, memory, cache_kv, dense, own, recalled,
           peak_at, total_at, summed_at):
    pieces, slots = cache_kv.shape[0], cache_kv.shape[1]
    tile = (ROWS, DH)
    row, lane = iota(tile, 0), iota(tile, 1)
    eye = row == lane

    empty = jnp.where(row == M_ROW, masked_score, 0.0).astype(f32)
    dense[...] = jnp.broadcast_to(empty[None], dense.shape)
    for s in range(pieces):
        r = owner[s]
        peak_at[r] = jnp.full(tile, masked_score, f32)
        total_at[r] = jnp.zeros(tile, f32)
        summed_at[r] = jnp.zeros(tile, f32)

    slot = iota((ROWS, slots), 1)
    parts = []
    for s in range(pieces):
        valid = slot < length[s]
        score = jnp.where(valid, dot_t(query_all[owner[s]], cache_kv[s, :, :DH]), masked_score)
        peak = jnp.max(score, axis=-1, keepdims=True)
        weight = jnp.where(valid, jnp.exp(score - peak), 0.0)
        total = jnp.sum(weight, axis=-1, keepdims=True)
        parts.append((peak, total, dot(weight.astype(bf16), cache_kv[s, :, DH:])))

    q = query[...]
    score_persist = dot_t(q, persist_kv[:, :DH])
    score_new = dot_t(q, new_kv[:, :DH])
    causal = iota((ROWS, ROWS), 0) >= iota((ROWS, ROWS), 1)
    score_new = jnp.where(causal, score_new, masked_score)
    peak = jnp.maximum(
        jnp.max(score_persist, axis=-1, keepdims=True), jnp.max(score_new, axis=-1, keepdims=True)
    )
    weight_persist = jnp.exp(score_persist - peak)
    weight_new = jnp.exp(score_new - peak)
    total = jnp.sum(weight_persist, axis=-1, keepdims=True) + jnp.sum(weight_new, axis=-1, keepdims=True)
    summed = dot(weight_persist.astype(bf16), persist_kv[:, DH:])
    summed = summed + dot(weight_new.astype(bf16), new_kv[:, DH:])
    own[...] = packed(jnp.broadcast_to(peak, tile), jnp.broadcast_to(total, tile), summed, eye, row)
    recalled[...] = dot(q, memory[...])

    for s in range(pieces):
        r = owner[s]
        peak, total, summed = parts[s]
        before = peak_at[r]
        joint = jnp.maximum(before, peak)
        scale_before = jnp.exp(before - joint)
        scale = jnp.exp(peak - joint)
        peak_at[r] = joint
        total_at[r] = total_at[r] * scale_before + total * scale
        summed_at[r] = summed_at[r] * scale_before + summed * scale
    for s in range(pieces):
        r = owner[s]
        dense[r] = packed(peak_at[r], total_at[r], summed_at[r], eye, row)


def merge(received, own, recalled, w_out, partial_out):
    tile = (ROWS, DH)
    row, lane = iota(tile, 0), iota(tile, 1)
    eye = row == lane
    sources = received.shape[0]
    blocks = [own[...]] + [received[s] for s in range(sources)]
    top = blocks[0]
    for block in blocks[1:]:
        top = jnp.maximum(top, block)
    peak = top[M_ROW : M_ROW + 1]
    summed = jnp.zeros(tile, f32)
    total = jnp.zeros((1, DH), f32)
    for block in blocks:
        scale = jnp.exp(block[M_ROW : M_ROW + 1] - peak)
        total = total + block[L_ROW : L_ROW + 1] * scale
        summed = summed + block * to_col(scale, eye)
    attended = summed / to_col(total, eye)
    head_out = jnp.where(row < Q, attended + recalled[...], 0.0).astype(bf16)
    terms = dot(head_out, w_out[...])
    for h in range(partial_out.shape[0]):
        partial_out[h] = terms[:, h * DH : (h + 1) * DH]


def vmem(n):
    return [pl.BlockSpec(memory_space=pltpu.VMEM)] * n


def smem(n):
    return [pl.BlockSpec(memory_space=pltpu.SMEM)] * n


def shards(tokens, norm_gain, w_qkv, persist_kv, memory, cache_kv, piece_owner, piece_len, w_out):
    total_reqs = lax.axis_size("req")
    heads = lax.axis_size("head")
    d = tokens.shape[1]
    pieces, slots = cache_kv.shape[:2]
    tile = (ROWS, DH)
    dense_shape = (total_reqs,) + tile

    query_all, query, new_kv = pl.pallas_call(
        project,
        out_shape=(
            jax.ShapeDtypeStruct(dense_shape, bf16),
            jax.ShapeDtypeStruct(tile, bf16),
            jax.ShapeDtypeStruct((ROWS, 2 * DH), bf16),
        ),
        in_specs=vmem(3),
        out_specs=tuple(vmem(3)),
        scratch_shapes=[pltpu.VMEM((ROWS, 3 * DH), f32)],
        name="project",
    )(tokens, norm_gain.reshape(1, d), w_qkv.reshape(d, 3 * DH))

    query_all = lax.all_to_all(query_all, "req", 0, 0, tiled=True)

    dense, own, recalled = pl.pallas_call(
        attend,
        out_shape=(
            jax.ShapeDtypeStruct(dense_shape, f32),
            jax.ShapeDtypeStruct(tile, f32),
            jax.ShapeDtypeStruct(tile, f32),
        ),
        in_specs=smem(2) + vmem(6),
        out_specs=tuple(vmem(3)),
        scratch_shapes=[pltpu.VMEM(dense_shape, f32)] * 3,
        name="attend",
    )(
        piece_owner,
        piece_len,
        query_all,
        query,
        new_kv,
        persist_kv.reshape(NP, 2 * DH),
        memory.reshape(DH, DH),
        cache_kv.reshape(pieces, slots, 2 * DH),
    )

    received = lax.all_to_all(dense, "req", 0, 0, tiled=True)

    partial_out = pl.pallas_call(
        merge,
        out_shape=jax.ShapeDtypeStruct((heads,) + tile, f32),
        in_specs=vmem(4),
        out_specs=vmem(1)[0],
        name="merge",
    )(received, own, recalled, w_out.reshape(DH, d))

    terms = lax.all_to_all(partial_out, "head", 0, 0, tiled=True)
    return jnp.sum(terms, axis=0)[:Q].astype(bf16)


def solution(mesh):
    in_specs = (
        P("req", None),
        P(),
        P(None, "head", None),
        P("head", None, None),
        P("req", "head", None, None),
        P("req", None, "head", None),
        P("req"),
        P("req"),
        P("head", None, None),
    )
    out_specs = P("req", "head")
    return jax.shard_map(shards, mesh=mesh, in_specs=in_specs, out_specs=out_specs, check_vma=False)
```

time: 406 us -> 81.7 us (0.20)
  blocking collectives: 202 us -> 72 us
  waiting for transfers between devices: 79.8 us -> 0 us
  local copies, waits for them, and re-layouts: 74.2 us -> 0 us
  other arithmetic: 25.4 us -> 0.59 us
  between operations: 13.6 us -> 0.01 us
  Pallas kernels: 0 us -> 8.67 us
  matrix products: 5.77 us -> 0 us
    all_gather x3 -> x0, blocking collectives: 202 us -> none  [the longest x2 132 us: merged(): everything = jax.tree.map(lambda part: lax.all_gather(part, axis), shard)]
    all_to_all x0 -> x3, blocking collectives: none -> 72 us  [the longest x1 33.2 us: shards(): query_all = lax.all_to_all(query_all, 'req', 0, 0, tiled=True)]
    dynamic_slice x63 -> x0, local copies, waits for them, and re-layouts: 59.1 us -> none  [step(): return combine(so_far, jax.tree.map(lambda part: part[k], everything))]
    reduce_scatter x1 -> x0, waiting for transfers between devices: 40.5 us -> none  [shards(): lax.psum_scatter(partial_out, 'head', scatter_dimension=1, tiled=True)]
    all_gather x1 -> x0, waiting for transfers between devices: 39.2 us -> none  [merged(): everything = jax.tree.map(lambda part: lax.all_gather(part, axis), shard)]
    add x126 -> x0, other arithmetic: 20 us -> none  [the longest x63 17.9 us: join_parts(): summed = first[2] * scale_one[..., None] + second[2] * scale_two[..., None]]
    mul x126 -> x0, local copies, waits for them, and re-layouts: 12.1 us -> none  [join_parts(): summed = first[2] * scale_one[..., None] + second[2] * scale_two[..., None]]
    pallas_call x0 -> x3, Pallas kernels: none -> 8.67 us  [the longest x1 4.57 us: shards(): pl.pallas_call(attend, out_shape=(jax.ShapeDtypeStruct(dense_shape, f32),...]
  transfers between devices with their start and end apart: 2 -> 0, of which waited for: 2 -> 0; matrix products, arithmetic and copies ran while one was open for 0% -> 0% of each run, Pallas kernels for 0% -> 0%
where the time goes in v1:
time: 81.7 us; the launch traced here: 81.3 us
  blocking collectives  72 us (88%)
  Pallas kernels  8.67 us (11%)
    all_to_all x1, blocking collectives, shards(): query_all = lax.all_to_all(query_all, 'req', 0, 0, tiled=True)  33.2 us
    all_to_all x1, blocking collectives, shards(): received = lax.all_to_all(dense, 'req', 0, 0, tiled=True)  26.4 us
    all_to_all x1, blocking collectives, shards(): terms = lax.all_to_all(partial_out, 'head', 0, 0, tiled=True)  12.5 us
    pallas_call x1, Pallas kernels, shards(): pl.pallas_call(attend, out_shape=(jax.ShapeDtypeStruct(dense_shape, f32),...  4.57 us
    pallas_call x1, Pallas kernels, shards(): pl.pallas_call(project, out_shape=(jax.ShapeDtypeStruct(dense_shape, bf16...  2.1 us
    pallas_call x1, Pallas kernels, shards(): pl.pallas_call(merge, out_shape=jax.ShapeDtypeStruct((heads,) + tile, f32...  2 us

profile of v1, /device:TPU:1, one launch (start us, length us, event | category | flops | bytes accessed | tf_op | source)
XLA Modules:
  0.0 81.3 jit_solution(7829664679861423532)
XLA Ops:
  0.0 2.1 %project.1 = (bf16[64,8,128]{2,1,0:T(8,128)(2,1)}, bf16[8,128]{1,0:T(8,128)(2,1)}, bf16[8,256]{1,0:T(8,128)(2,1)}) custom-call(bf16[5,1024]{1,0:T(8,128)(2,1)} %tokens.1, f32[1,1024]{1,0:T(1,128)} %bitcast.12, bf16[1024,384]{1,0:T(8,128)(2,1)} %bitcast.8), custom_call_target="tpu_custom_call" | custom-call | tf_op jit(solution)/shard_map/project/pallas_call | solution.py:154
  2.1 33.2 %all_to_all.15.query_all = bf16[64,8,128]{2,1,0:T(8,128)(2,1)} all-to-all(bf16[64,8,128]{2,1,0:T(8,128)(2,1)} %get-tuple-element.11), channel_id=1, replica_groups=mesh['req'=64,'head'=8] {'req'}, dimensions={0} | all-to-all | bytes 262144 | tf_op jit(solution)/shard_map/all_to_all | solution.py:167
  35.3 4.6 %attend.1 = (f32[64,8,128]{2,1,0:T(8,128)}, f32[8,128]{1,0:T(8,128)}, f32[8,128]{1,0:T(8,128)}) custom-call(s32[8]{0:T(128)} %owner.1, s32[8]{0:T(128)} %length.1, bf16[64,8,128]{2,1,0:T(8,128)(2,1)} %all_to_all.15.query_all, bf16[8,128]{1,0:T(8,128)(2,1)} %get-tuple-element.12.query, bf16[8,256]{1,0:T(8,128)(2,1)} %get-tuple-element.13.new_kv, ...), custom_call_target="tpu_custom_call" | custom-call | tf_op jit(solution)/shard_map/attend/pallas_call | solution.py:169
  39.9 26.4 %all_to_all.16.received = f32[64,8,128]{2,1,0:T(8,128)} all-to-all(f32[64,8,128]{2,1,0:T(8,128)} %get-tuple-element.14), channel_id=1, replica_groups=mesh['req'=64,'head'=8] {'req'}, dimensions={0} | all-to-all | bytes 524288 | tf_op jit(solution)/shard_map/all_to_all | solution.py:191
  66.3 2.0 %merge.1 = f32[8,8,128]{2,1,0:T(8,128)} custom-call(f32[64,8,128]{2,1,0:T(8,128)} %all_to_all.16.received, f32[8,128]{1,0:T(8,128)} %get-tuple-element.15.own, f32[8,128]{1,0:T(8,128)} %get-tuple-element.16.recalled, bf16[128,1024]{1,0:T(8,128)(2,1)} %bitcast.9), custom_call_target="tpu_custom_call" | custom-call | tf_op jit(solution)/shard_map/merge/pallas_call | solution.py:193
  68.3 12.5 %all_to_all.17 = f32[8,8,128]{2,1,0:T(8,128)S(1)} all-to-all(f32[8,8,128]{2,1,0:T(8,128)} %merge.1), channel_id=1, replica_groups=mesh['req'=64,'head'=8] {'head'}, dimensions={0} | all-to-all | bytes 65536 | tf_op jit(solution)/shard_map/all_to_all | solution.py:201
  80.7 0.6 reduce_sum.9

commit v2 on v1

--- a/solution.py
+++ b/solution.py
@@ -9,11 +9,10 @@
 NP = 16
 Q = 5
 ROWS = 8
-M_ROW = 5
-L_ROW = 6
 
 masked_score = -1e30
 norm_eps = 1e-06
+kernel_vmem = 8 << 20
 f32 = jnp.float32
 bf16 = jnp.bfloat16
 
@@ -30,20 +29,32 @@
     return lax.dot_general(a, b, (((1,), (1,)), ((), ())), preferred_element_type=f32)
 
 
-def to_row(col, eye):
-    return jnp.sum(jnp.where(eye, col, 0.0), axis=0, keepdims=True)
-
-
-def to_col(row, eye):
-    return jnp.sum(jnp.where(eye, jnp.broadcast_to(row, eye.shape), 0.0), axis=1, keepdims=True)
-
-
-def packed(peak, total, summed, eye, row):
-    tail = jnp.where(row == M_ROW, to_row(peak, eye), to_row(total, eye))
-    return jnp.where(row < Q, summed, tail)
-
-
-def project(tokens, gain, w_qkv, query_all, query, new_kv, padded):
+def stats_row(peak, total, row, lane):
+    picked = jnp.where(lane == row, peak, jnp.where(lane == row + ROWS, total, 0.0))
+    return jnp.sum(picked, axis=0, keepdims=True)
+
+
+def to_col(values, row, lane):
+    spread = jnp.broadcast_to(values, row.shape)
+    return jnp.sum(jnp.where(row == lane, spread, 0.0), axis=1, keepdims=True)
+
+
+def packed(peak, total, summed, row, lane):
+    stats = stats_row(peak, total, row, lane)
+    high = stats.astype(bf16).astype(f32)
+    rest = stats - high
+    middle = rest.astype(bf16).astype(f32)
+    low = rest - middle
+    tail = jnp.where(row == Q, high, jnp.where(row == Q + 1, middle, low))
+    return jnp.where(row < Q, summed, tail).astype(bf16)
+
+
+def project(tokens, gain, w_qkv, cache_kv, persist_kv, memory, w_out, query_all, query, new_kv,
+            cache_here, persist_here, memory_here, w_out_here, padded, sems):
+    pairs = ((cache_kv, cache_here), (persist_kv, persist_here), (memory, memory_here), (w_out, w_out_here))
+    copies = [pltpu.make_async_copy(a, b, sems.at[i]) for i, (a, b) in enumerate(pairs)]
+    for copy in copies:
+        copy.start()
     xf = tokens[...].astype(f32)
     inverse = lax.rsqrt(jnp.mean(xf * xf, axis=-1, keepdims=True) + norm_eps)
     normed = (xf * inverse * gain[...]).astype(bf16)
@@ -54,6 +65,8 @@
     query[...] = q
     query_all[...] = jnp.broadcast_to(q[None], query_all.shape)
     new_kv[...] = proj[:, DH:].astype(bf16)
+    for copy in copies:
+        copy.wait()
 
 
 def attend(owner, length, query_all, query, new_kv, persist_kv, memory, cache_kv, dense, own, recalled,
@@ -61,9 +74,8 @@
     pieces, slots = cache_kv.shape[0], cache_kv.shape[1]
     tile = (ROWS, DH)
     row, lane = iota(tile, 0), iota(tile, 1)
-    eye = row == lane
-
-    empty = jnp.where(row == M_ROW, masked_score, 0.0).astype(f32)
+
+    empty = jnp.where((row == Q) & (lane < ROWS), masked_score, 0.0).astype(bf16)
     dense[...] = jnp.broadcast_to(empty[None], dense.shape)
     for s in range(pieces):
         r = owner[s]
@@ -94,7 +106,8 @@
     total = jnp.sum(weight_persist, axis=-1, keepdims=True) + jnp.sum(weight_new, axis=-1, keepdims=True)
     summed = dot(weight_persist.astype(bf16), persist_kv[:, DH:])
     summed = summed + dot(weight_new.astype(bf16), new_kv[:, DH:])
-    own[...] = packed(jnp.broadcast_to(peak, tile), jnp.broadcast_to(total, tile), summed, eye, row)
+    stats = stats_row(jnp.broadcast_to(peak, tile), jnp.broadcast_to(total, tile), row, lane)
+    own[...] = jnp.where(row < Q, summed, jnp.where(row == Q, stats, 0.0))
     recalled[...] = dot(q, memory[...])
 
     for s in range(pieces):
@@ -109,30 +122,34 @@
         summed_at[r] = summed_at[r] * scale_before + summed * scale
     for s in range(pieces):
         r = owner[s]
-        dense[r] = packed(peak_at[r], total_at[r], summed_at[r], eye, row)
+        dense[r] = packed(peak_at[r], total_at[r], summed_at[r], row, lane)
 
 
 def merge(received, own, recalled, w_out, partial_out):
     tile = (ROWS, DH)
     row, lane = iota(tile, 0), iota(tile, 1)
-    eye = row == lane
     sources = received.shape[0]
-    blocks = [own[...]] + [received[s] for s in range(sources)]
-    top = blocks[0]
-    for block in blocks[1:]:
-        top = jnp.maximum(top, block)
-    peak = top[M_ROW : M_ROW + 1]
+    blocks = [own[...]] + [received[s].astype(f32) for s in range(sources)]
+    stats = [jnp.sum(jnp.where(row >= Q, block, 0.0), axis=0, keepdims=True) for block in blocks]
+    peak = stats[0]
+    for each in stats[1:]:
+        peak = jnp.maximum(peak, each)
     summed = jnp.zeros(tile, f32)
-    total = jnp.zeros((1, DH), f32)
-    for block in blocks:
-        scale = jnp.exp(block[M_ROW : M_ROW + 1] - peak)
-        total = total + block[L_ROW : L_ROW + 1] * scale
-        summed = summed + block * to_col(scale, eye)
-    attended = summed / to_col(total, eye)
+    total = jnp.zeros((ROWS, 1), f32)
+    for block, each in zip(blocks, stats):
+        scale = jnp.exp(each - peak)
+        col = to_col(scale, row, lane)
+        total = total + col * to_col(each, row, lane - ROWS)
+        summed = summed + block * col
+    attended = summed / total
     head_out = jnp.where(row < Q, attended + recalled[...], 0.0).astype(bf16)
     terms = dot(head_out, w_out[...])
     for h in range(partial_out.shape[0]):
         partial_out[h] = terms[:, h * DH : (h + 1) * DH]
+
+
+def held_in(space, *arrays):
+    return [pltpu.with_memory_space_constraint(x, space) for x in arrays]
 
 
 def vmem(n):
@@ -151,52 +168,49 @@
     tile = (ROWS, DH)
     dense_shape = (total_reqs,) + tile
 
-    query_all, query, new_kv = pl.pallas_call(
+    cache_kv = cache_kv.reshape(pieces, slots, 2 * DH)
+    persist_kv = persist_kv.reshape(NP, 2 * DH)
+    memory = memory.reshape(DH, DH)
+    w_out = w_out.reshape(DH, d)
+    fetched = (cache_kv, persist_kv, memory, w_out)
+    query_all, query, new_kv, *fetched = pl.pallas_call(
         project,
         out_shape=(
-            jax.ShapeDtypeStruct(dense_shape, bf16),
-            jax.ShapeDtypeStruct(tile, bf16),
-            jax.ShapeDtypeStruct((ROWS, 2 * DH), bf16),
+            pltpu.VMEM(dense_shape, bf16),
+            pltpu.VMEM(tile, bf16),
+            pltpu.VMEM((ROWS, 2 * DH), bf16),
+            *(pltpu.VMEM(x.shape, x.dtype) for x in fetched),
         ),
-        in_specs=vmem(3),
-        out_specs=tuple(vmem(3)),
-        scratch_shapes=[pltpu.VMEM((ROWS, 3 * DH), f32)],
+        in_specs=vmem(3) + [pl.BlockSpec(memory_space=pl.ANY)] * len(fetched),
+        out_specs=tuple(vmem(3 + len(fetched))),
+        scratch_shapes=[pltpu.VMEM((ROWS, 3 * DH), f32), pltpu.SemaphoreType.DMA((len(fetched),))],
+        compiler_params=pltpu.CompilerParams(vmem_limit_bytes=kernel_vmem),
         name="project",
-    )(tokens, norm_gain.reshape(1, d), w_qkv.reshape(d, 3 * DH))
+    )(*held_in(pltpu.HBM, tokens, norm_gain.reshape(1, d), w_qkv.reshape(d, 3 * DH), *fetched))
+    cache_kv, persist_kv, memory, w_out = fetched
 
     query_all = lax.all_to_all(query_all, "req", 0, 0, tiled=True)
 
     dense, own, recalled = pl.pallas_call(
         attend,
-        out_shape=(
-            jax.ShapeDtypeStruct(dense_shape, f32),
-            jax.ShapeDtypeStruct(tile, f32),
-            jax.ShapeDtypeStruct(tile, f32),
-        ),
+        out_shape=(pltpu.VMEM(dense_shape, bf16), pltpu.VMEM(tile, f32), pltpu.VMEM(tile, f32)),
         in_specs=smem(2) + vmem(6),
         out_specs=tuple(vmem(3)),
         scratch_shapes=[pltpu.VMEM(dense_shape, f32)] * 3,
+        compiler_params=pltpu.CompilerParams(vmem_limit_bytes=kernel_vmem),
         name="attend",
-    )(
-        piece_owner,
-        piece_len,
-        query_all,
-        query,
-        new_kv,
-        persist_kv.reshape(NP, 2 * DH),
-        memory.reshape(DH, DH),
-        cache_kv.reshape(pieces, slots, 2 * DH),
-    )
+    )(*held_in(pltpu.HBM, piece_owner, piece_len), *held_in(pltpu.VMEM, query_all, query, new_kv, persist_kv, memory, cache_kv))
 
     received = lax.all_to_all(dense, "req", 0, 0, tiled=True)
 
     partial_out = pl.pallas_call(
         merge,
-        out_shape=jax.ShapeDtypeStruct((heads,) + tile, f32),
+        out_shape=pltpu.VMEM((heads,) + tile, f32),
         in_specs=vmem(4),
         out_specs=vmem(1)[0],
+        compiler_params=pltpu.CompilerParams(vmem_limit_bytes=kernel_vmem),
         name="merge",
-    )(received, own, recalled, w_out.reshape(DH, d))
+    )(*held_in(pltpu.VMEM, received, own, recalled, w_out))
 
     terms = lax.all_to_all(partial_out, "head", 0, 0, tiled=True)
     return jnp.sum(terms, axis=0)[:Q].astype(bf16)

time: 81.7 us -> 73.7 us (0.902)
  blocking collectives: 72 us -> 66.6 us
  Pallas kernels: 8.67 us -> 6.15 us
    all_to_all x1, blocking collectives: 26.4 us -> 21.4 us  [shards(): received = lax.all_to_all(dense, 'req', 0, 0, tiled=True)]
    pallas_call x3, Pallas kernels: 8.67 us -> 6.15 us  [the longest x1 2.88 us: shards(): pl.pallas_call(attend, out_shape=(pltpu.VMEM(dense_shape, bf16), pltpu.VM...]
where the time goes in v2:
time: 73.7 us; the launch traced here: 73.4 us
  blocking collectives  66.6 us (90%)
  Pallas kernels  6.15 us (8%)
    all_to_all x1, blocking collectives, shards(): query_all = lax.all_to_all(query_all, 'req', 0, 0, tiled=True)  32.9 us
    all_to_all x1, blocking collectives, shards(): received = lax.all_to_all(dense, 'req', 0, 0, tiled=True)  21.4 us
    all_to_all x1, blocking collectives, shards(): terms = lax.all_to_all(partial_out, 'head', 0, 0, tiled=True)  12.4 us
    pallas_call x1, Pallas kernels, shards(): pl.pallas_call(attend, out_shape=(pltpu.VMEM(dense_shape, bf16), pltpu.VM...  2.88 us
    pallas_call x1, Pallas kernels, shards(): pl.pallas_call(project, out_shape=(pltpu.VMEM(dense_shape, bf16), pltpu.V...  2.83 us

profile of v2, /device:TPU:1, one launch (start us, length us, event | category | flops | bytes accessed | tf_op | source)
XLA Modules:
  0.0 73.4 jit_solution(15506252766039181475)
XLA Ops:
  0.0 2.8 %project.1 = (bf16[64,8,128]{2,1,0:T(8,128)(2,1)S(1)}, bf16[8,128]{1,0:T(8,128)(2,1)S(1)}, bf16[8,256]{1,0:T(8,128)(2,1)S(1)}, bf16[8,512,256]{2,1,0:T(8,128)(2,...) custom-call(bf16[5,1024]{1,0:T(8,128)(2,1)} %tokens.1, ...), custom_call_target="tpu_custom_call" | custom-call | tf_op jit(solution)/shard_map/project/pallas_call | solution.py:176
  2.8 32.9 %all_to_all.15.query_all = bf16[64,8,128]{2,1,0:T(8,128)(2,1)S(1)} all-to-all(bf16[64,8,128]{2,1,0:T(8,128)(2,1)S(1)} %get-tuple-element.15), channel_id=1, replica_groups=mesh['req'=64,'head'=8] {'req'}, dimensions={0} | all-to-all | bytes 262144 | tf_op jit(solution)/shard_map/all_to_all | solution.py:192
  35.7 2.9 %attend.1 = (bf16[64,8,128]{2,1,0:T(8,128)(2,1)S(1)}, f32[8,128]{1,0:T(8,128)S(1)}, f32[8,128]{1,0:T(8,128)S(1)}) custom-call(s32[8]{0:T(128)} %owner.1, s32[8]{0:T(128)} %length.1, bf16[64,8,128]{2,1,0:T(8,128)(2,1)S(1)} %all_to_all.15.query_all, bf16[8,128]{1,0:T(8,128)(2,1)S(1)} %get-tuple-element.16.query, bf16[8,256]{1,0:T(8,128)(2,1)S(1)} %get-tuple-element.17.new_kv, ...), custom_call_target="tpu_custom_call" | custom-call | tf_op jit(solution)/shard_map/attend/pallas_call | solution.py:194
  38.6 21.4 %all_to_all.16.received = bf16[64,8,128]{2,1,0:T(8,128)(2,1)S(1)} all-to-all(bf16[64,8,128]{2,1,0:T(8,128)(2,1)S(1)} %get-tuple-element.21), channel_id=1, replica_groups=mesh['req'=64,'head'=8] {'req'}, dimensions={0} | all-to-all | bytes 262144 | tf_op jit(solution)/shard_map/all_to_all | solution.py:204
  60.0 0.4 merge.1
  60.4 12.4 %all_to_all.17 = f32[8,8,128]{2,1,0:T(8,128)S(1)} all-to-all(f32[8,8,128]{2,1,0:T(8,128)S(1)} %merge.1), channel_id=1, replica_groups=mesh['req'=64,'head'=8] {'head'}, dimensions={0} | all-to-all | bytes 65536 | tf_op jit(solution)/shard_map/all_to_all | solution.py:215
  72.8 0.6 reduce_sum.9

commit v3 on v2

v3 whole, which is shorter than its diff:
```python
import functools

import jax
import jax.numpy as jnp
from jax import lax
from jax.experimental import pallas as pl
from jax.experimental.pallas import tpu as pltpu
from jax.sharding import Mesh
from jax.sharding import PartitionSpec as P

DH = 128
NP = 16
Q = 5
ROWS = 8

masked_score = -1e30
norm_eps = 1e-06
kernel_vmem = 8 << 20
f32 = jnp.float32
bf16 = jnp.bfloat16


def iota(shape, axis):
    return lax.broadcasted_iota(jnp.int32, shape, axis)


def dot(a, b):
    return jnp.dot(a, b, preferred_element_type=f32)


def dot_t(a, b):
    return lax.dot_general(a, b, (((1,), (1,)), ((), ())), preferred_element_type=f32)


def stats_row(peak, total, row, lane):
    picked = jnp.where(lane == row, peak, jnp.where(lane == row + ROWS, total, 0.0))
    return jnp.sum(picked, axis=0, keepdims=True)


def to_col(values, row, lane):
    spread = jnp.broadcast_to(values, row.shape)
    return jnp.sum(jnp.where(row == lane, spread, 0.0), axis=1, keepdims=True)


def packed(peak, total, summed, row, lane):
    stats = stats_row(peak, total, row, lane)
    high = stats.astype(bf16).astype(f32)
    rest = stats - high
    middle = rest.astype(bf16).astype(f32)
    low = rest - middle
    tail = jnp.where(row == Q, high, jnp.where(row == Q + 1, middle, low))
    return jnp.where(row < Q, summed, tail).astype(bf16)


def project(tokens, gain, w_query, query_all, query, normed, padded):
    xf = tokens[...].astype(f32)
    inverse = lax.rsqrt(jnp.mean(xf * xf, axis=-1, keepdims=True) + norm_eps)
    normed[...] = (xf * inverse * gain[...]).astype(bf16)
    padded[...] = jnp.zeros_like(padded)
    padded[0:Q, :] = dot(normed[...], w_query[...])
    q = (padded[...] * DH ** (-0.5)).astype(bf16)
    query[...] = q
    query_all[...] = jnp.broadcast_to(q[None], query_all.shape)


def own_part(rows, columns, normed, query, w_key, w_value, persist_kv, memory, cache_kv, w_out, owner, length,
             own, recalled, cache_here, w_out_here, place, length_here, padded, owner_here, sems):
    pairs = ((owner, owner_here), (length, length_here), (cache_kv, cache_here), (w_out, w_out_here))
    copies = [pltpu.make_async_copy(a, b, sems.at[i]) for i, (a, b) in enumerate(pairs)]
    for copy in copies:
        copy.start()
    tile = (ROWS, DH)
    row, lane = iota(tile, 0), iota(tile, 1)
    padded[...] = jnp.zeros_like(padded)
    padded[0:Q, :DH] = dot(normed[...], w_key[...])
    padded[0:Q, DH:] = dot(normed[...], w_value[...])
    new_kv = padded[...].astype(bf16)
    q = query[...]
    score_persist = dot_t(q, persist_kv[:, :DH])
    score_new = dot_t(q, new_kv[:, :DH])
    causal = iota((ROWS, ROWS), 0) >= iota((ROWS, ROWS), 1)
    score_new = jnp.where(causal, score_new, masked_score)
    peak = jnp.maximum(
        jnp.max(score_persist, axis=-1, keepdims=True), jnp.max(score_new, axis=-1, keepdims=True)
    )
    weight_persist = jnp.exp(score_persist - peak)
    weight_new = jnp.exp(score_new - peak)
    total = jnp.sum(weight_persist, axis=-1, keepdims=True) + jnp.sum(weight_new, axis=-1, keepdims=True)
    summed = dot(weight_persist.astype(bf16), persist_kv[:, DH:])
    summed = summed + dot(weight_new.astype(bf16), new_kv[:, DH:])
    stats = stats_row(jnp.broadcast_to(peak, tile), jnp.broadcast_to(total, tile), row, lane)
    own[...] = jnp.where(row < Q, summed, jnp.where(row == Q, stats, 0.0))
    recalled[...] = dot(q, memory[...])
    for copy in copies:
        copy.wait()
    for s in range(place.shape[0]):
        r = owner_here[s]
        place[s] = lax.rem(r, columns) * rows + lax.div(r, columns)


def attend(place, length, query_all, cache_kv, dense, peak_at, total_at, summed_at):
    pieces, slots = cache_kv.shape[0], cache_kv.shape[1]
    tile = (ROWS, DH)
    row, lane = iota(tile, 0), iota(tile, 1)

    empty = jnp.where((row == Q) & (lane < ROWS), masked_score, 0.0).astype(bf16)
    dense[...] = jnp.broadcast_to(empty[None], dense.shape)
    for s in range(pieces):
        r = place[s]
        peak_at[r] = jnp.full(tile, masked_score, f32)
        total_at[r] = jnp.zeros(tile, f32)
        summed_at[r] = jnp.zeros(tile, f32)

    slot = iota((ROWS, slots), 1)
    parts = []
    for s in range(pieces):
        valid = slot < length[s]
        score = jnp.where(valid, dot_t(query_all[place[s]], cache_kv[s, :, :DH]), masked_score)
        peak = jnp.max(score, axis=-1, keepdims=True)
        weight = jnp.where(valid, jnp.exp(score - peak), 0.0)
        total = jnp.sum(weight, axis=-1, keepdims=True)
        parts.append((peak, total, dot(weight.astype(bf16), cache_kv[s, :, DH:])))

    for s in range(pieces):
        r = place[s]
        peak, total, summed = parts[s]
        before = peak_at[r]
        joint = jnp.maximum(before, peak)
        scale_before = jnp.exp(before - joint)
        scale = jnp.exp(peak - joint)
        peak_at[r] = joint
        total_at[r] = total_at[r] * scale_before + total * scale
        summed_at[r] = summed_at[r] * scale_before + summed * scale
    for s in range(pieces):
        r = place[s]
        dense[r] = packed(peak_at[r], total_at[r], summed_at[r], row, lane)


def merge(received, own, recalled, w_out, partial_out):
    tile = (ROWS, DH)
    row, lane = iota(tile, 0), iota(tile, 1)
    sources = received.shape[0]
    blocks = [own[...]] + [received[s].astype(f32) for s in range(sources)]
    stats = [jnp.sum(jnp.where(row >= Q, block, 0.0), axis=0, keepdims=True) for block in blocks]
    peak = stats[0]
    for each in stats[1:]:
        peak = jnp.maximum(peak, each)
    summed = jnp.zeros(tile, f32)
    total = jnp.zeros((ROWS, 1), f32)
    for block, each in zip(blocks, stats):
        scale = jnp.exp(each - peak)
        col = to_col(scale, row, lane)
        total = total + col * to_col(each, row, lane - ROWS)
        summed = summed + block * col
    attended = summed / total
    head_out = jnp.where(row < Q, attended + recalled[...], 0.0).astype(bf16)
    terms = dot(head_out, w_out[...])
    for h in range(partial_out.shape[0]):
        partial_out[h] = terms[:, h * DH : (h + 1) * DH]


def held_in(space, *arrays):
    return [pltpu.with_memory_space_constraint(x, space) for x in arrays]


def vmem(n):
    return [pl.BlockSpec(memory_space=pltpu.VMEM)] * n


def smem(n):
    return [pl.BlockSpec(memory_space=pltpu.SMEM)] * n


def hbm(n):
    return [pl.BlockSpec(memory_space=pl.ANY)] * n


def column_block(d, j):
    return pl.BlockSpec((d, DH), lambda i: (0, j))


def shards(tokens, norm_gain, w_qkv, persist_kv, memory, cache_kv, piece_owner, piece_len, w_out):
    rows, columns = lax.axis_size("x"), lax.axis_size("z")
    heads = lax.axis_size("head")
    d = tokens.shape[1]
    pieces, slots = cache_kv.shape[:2]
    tile = (ROWS, DH)
    dense_shape = (rows * columns,) + tile
    params = pltpu.CompilerParams(vmem_limit_bytes=kernel_vmem)

    w_qkv, persist_kv, memory, cache_kv, w_out, piece_owner, piece_len = held_in(
        pltpu.HBM,
        w_qkv.reshape(d, 3 * DH),
        persist_kv.reshape(NP, 2 * DH),
        memory.reshape(DH, DH),
        cache_kv.reshape(pieces, slots, 2 * DH),
        w_out.reshape(DH, d),
        piece_owner,
        piece_len,
    )
    query_all, query, normed = pl.pallas_call(
        project,
        grid=(1,),
        out_shape=(pltpu.VMEM(dense_shape, bf16), pltpu.VMEM(tile, bf16), pltpu.VMEM(tokens.shape, bf16)),
        in_specs=vmem(2) + [column_block(d, 0)],
        out_specs=tuple(vmem(3)),
        scratch_shapes=[pltpu.VMEM(tile, f32)],
        compiler_params=params,
        name="project",
    )(*held_in(pltpu.HBM, tokens, norm_gain.reshape(1, d)), w_qkv)

    query_all = lax.all_to_all(query_all, ("z", "x"), 0, 0, tiled=True)

    own, recalled, cache_kv, w_out, place, piece_len = pl.pallas_call(
        functools.partial(own_part, rows, columns),
        grid=(1,),
        out_shape=(
            pltpu.VMEM(tile, f32),
            pltpu.VMEM(tile, f32),
            pltpu.VMEM(cache_kv.shape, bf16),
            pltpu.VMEM(w_out.shape, bf16),
            pltpu.SMEM((pieces,), jnp.int32),
            pltpu.SMEM((pieces,), jnp.int32),
        ),
        in_specs=vmem(2) + [column_block(d, 1), column_block(d, 2)] + vmem(2) + hbm(4),
        out_specs=tuple(vmem(4) + smem(2)),
        scratch_shapes=[
            pltpu.VMEM((ROWS, 2 * DH), f32),
            pltpu.SMEM((pieces,), jnp.int32),
            pltpu.SemaphoreType.DMA((4,)),
        ],
        compiler_params=params,
        name="own_part",
    )(*held_in(pltpu.VMEM, normed, query), w_qkv, w_qkv, persist_kv, memory, cache_kv, w_out, piece_owner, piece_len)

    dense = pl.pallas_call(
        attend,
        out_shape=pltpu.VMEM(dense_shape, bf16),
        in_specs=smem(2) + vmem(2),
        out_specs=vmem(1)[0],
        scratch_shapes=[pltpu.VMEM(dense_shape, f32)] * 3,
        compiler_params=params,
        name="attend",
    )(*held_in(pltpu.SMEM, place, piece_len), *held_in(pltpu.VMEM, query_all, cache_kv))

    received = lax.all_to_all(dense, ("z", "x"), 0, 0, tiled=True)

    partial_out = pl.pallas_call(
        merge,
        out_shape=pltpu.VMEM((heads,) + tile, f32),
        in_specs=vmem(4),
        out_specs=vmem(1)[0],
        compiler_params=params,
        name="merge",
    )(*held_in(pltpu.VMEM, received, own, recalled, w_out))

    terms = lax.all_to_all(partial_out, "head", 0, 0, tiled=True)
    return jnp.sum(terms, axis=0)[:Q].astype(bf16)


def solution(mesh):
    mesh = Mesh(mesh.devices.reshape(4, 16, 8), ("x", "z", "head"))
    req = ("x", "z")
    in_specs = (
        P(req, None),
        P(),
        P(None, "head", None),
        P("head", None, None),
        P(req, "head", None, None),
        P(req, None, "head", None),
        P(req),
        P(req),
        P("head", None, None),
    )
    out_specs = P(req, "head")
    return jax.shard_map(shards, mesh=mesh, in_specs=in_specs, out_specs=out_specs, check_vma=False)
```

time: 73.7 us -> 72.9 us (0.989)
  blocking collectives: 66.6 us -> 33.7 us
  starting transfers between devices: 0 us -> 19.1 us
  waiting for transfers between devices: 0 us -> 12.2 us
  Pallas kernels: 6.15 us -> 7 us
    all_to_all x2 -> x1, blocking collectives: 54.3 us -> 21.3 us  [shards(): received = lax.all_to_all(dense, ('z', 'x'), 0, 0, tiled=True)]
    all_to_all x0 -> x1, starting transfers between devices: none -> 19.1 us  [shards(): query_all = lax.all_to_all(query_all, ('z', 'x'), 0, 0, tiled=True)]
    all_to_all x0 -> x1, waiting for transfers between devices: none -> 12.2 us  [shards(): query_all = lax.all_to_all(query_all, ('z', 'x'), 0, 0, tiled=True)]
    pallas_call x2 -> x3, Pallas kernels: 5.71 us -> 6.56 us  [the longest x1 2.67 us: shards(): pl.pallas_call(functools.partial(own_part, rows, columns), grid=(1,), out...]
  transfers between devices with their start and end apart: 0 -> 1, of which waited for: 0 -> 1; matrix products, arithmetic and copies ran while one was open for 0% -> 0% of each run, Pallas kernels for 0% -> 4%
where the time goes in v3:
time: 72.9 us; the launch traced here: 72.6 us
  blocking collectives  33.7 us (46%)
  starting transfers between devices  19.1 us (26%)
  waiting for transfers between devices  12.2 us (17%)
  Pallas kernels  7 us (10%)
    all_to_all x1, blocking collectives, shards(): received = lax.all_to_all(dense, ('z', 'x'), 0, 0, tiled=True)  21.3 us
    all_to_all x1, starting transfers between devices, shards(): query_all = lax.all_to_all(query_all, ('z', 'x'), 0, 0, tiled=True)  19.1 us
    all_to_all x1, blocking collectives, shards(): terms = lax.all_to_all(partial_out, 'head', 0, 0, tiled=True)  12.4 us
    all_to_all x1, waiting for transfers between devices, shards(): query_all = lax.all_to_all(query_all, ('z', 'x'), 0, 0, tiled=True)  12.2 us
    pallas_call x1, Pallas kernels, shards(): pl.pallas_call(functools.partial(own_part, rows, columns), grid=(1,), out...  2.67 us
    pallas_call x1, Pallas kernels, shards(): pl.pallas_call(attend, out_shape=pltpu.VMEM(dense_shape, bf16), in_specs=...  2.01 us
    pallas_call x1, Pallas kernels, shards(): pl.pallas_call(project, grid=(1,), out_shape=(pltpu.VMEM(dense_shape, bf1...  1.87 us
  transfers between devices with their start and end apart: 1, of which 1 were waited for; matrix products, arithmetic and copies ran while one was open for 0% of the time, Pallas kernels for 4%

profile of v3, /device:TPU:1, one launch (start us, length us, event | category | flops | bytes accessed | tf_op | source)
XLA Modules:
  0.0 72.6 jit_solution(18363305069040873311)
XLA Ops:
  0.0 1.9 %project.1 = (bf16[64,8,128]{2,1,0:T(8,128)(2,1)}, bf16[8,128]{1,0:T(8,128)(2,1)S(1)}, bf16[5,1024]{1,0:T(8,128)(2,1)S(1)}) custom-call(bf16[5,1024]{1,0:T(8,128)(2,1)} %tokens.1, f32[1,1024]{1,0:T(1,128)} %bitcast.14, bf16[1024,384]{1,0:T(8,128)(2,1)} %bitcast.7), custom_call_target="tpu_custom_call" | custom-call | tf_op jit(solution)/shard_map/project/pallas_call | solution.py:201
  1.9 19.1 %all-to-all-start = ((bf16[64,8,128]{2,1,0:T(8,128)(2,1)}), bf16[64,8,128]{2,1,0:T(8,128)(2,1)S(1)}, u32[]{:S(2)}, u32[]{:S(2)}) async-start(bf16[64,8,128]{2,1,0:T(8,128)(2,1)} %get-tuple-element.18), calls=%async_computation | async-start | bytes 262144 | tf_op jit(solution)/shard_map/all_to_all | solution.py:212
  21.0 2.7 %own_part.1 = (f32[8,128]{1,0:T(8,128)S(1)}, f32[8,128]{1,0:T(8,128)S(1)}, bf16[8,512,256]{2,1,0:T(8,128)(2,1)S(1)}, bf16[128,1024]{1,0:T(8,128)(2,1)S(1)}, s32[8]{0:T(128)S(4)}, /*index=5*/s32[8]{0:T(128)S(4)}) custom-call(bf16[5,1024]{1,0:T(8,128)(2,1)S(1)} %get-tuple-element.14.normed, bf16[8,128]{1,0:T(8,128)(2,1)S(1)} %get-tuple-element.15.query, ...), custom_call_target="tpu_custom_call" | custom-call | tf_op jit(solution)/shard_map/own_part/pallas_call | solution.py:214
  23.7 12.2 %all-to-all-done.query_all = bf16[64,8,128]{2,1,0:T(8,128)(2,1)S(1)} async-done(((bf16[64,8,128]{2,1,0:T(8,128)(2,1)}), bf16[64,8,128]{2,1,0:T(8,128)(2,1)S(1)}, u32[]{:S(2)}, u32[]{:S(2)}) %all-to-all-start) | async-done | bytes 131104 | tf_op jit(solution)/shard_map/all_to_all | solution.py:212
  35.9 2.0 %attend.1 = bf16[64,8,128]{2,1,0:T(8,128)(2,1)S(1)} custom-call(s32[8]{0:T(128)S(4)} %get-tuple-element.16.place, s32[8]{0:T(128)S(4)} %get-tuple-element.17.length, bf16[64,8,128]{2,1,0:T(8,128)(2,1)S(1)} %all-to-all-done.query_all, bf16[8,512,256]{2,1,0:T(8,128)(2,1)S(1)} %get-tuple-element.19.cache_kv), custom_call_target="tpu_custom_call" | custom-call | tf_op jit(solution)/shard_map/attend/pallas_call | solution.py:236
  37.9 21.3 %all_to_all.15.received = bf16[64,8,128]{2,1,0:T(8,128)(2,1)S(1)} all-to-all(bf16[64,8,128]{2,1,0:T(8,128)(2,1)S(1)} %attend.1), channel_id=1, replica_groups=mesh['x'=4,'z'=16,'head'=8] {'z','x'}, dimensions={0} | all-to-all | bytes 262144 | tf_op jit(solution)/shard_map/all_to_all | solution.py:246
  59.2 0.4 merge.1
  59.7 12.4 %all_to_all.16 = f32[8,8,128]{2,1,0:T(8,128)S(1)} all-to-all(f32[8,8,128]{2,1,0:T(8,128)S(1)} %merge.1), channel_id=1, replica_groups=mesh['x'=4,'z'=16,'head'=8] {'head'}, dimensions={0} | all-to-all | bytes 65536 | tf_op jit(solution)/shard_map/all_to_all | solution.py:257
  72.1 0.6 reduce_sum.9
Async XLA Ops:
  1.9 34.0 %all-to-all-start = ((bf16[64,8,128]{2,1,0:T(8,128)(2,1)}), bf16[64,8,128]{2,1,0:T(8,128)(2,1)S(1)}, u32[]{:S(2)}, u32[]{:S(2)}) async-start(bf16[64,8,128]{2,1,0:T(8,128)(2,1)} %get-tuple-element.18), calls=%async_computation | async-start | bytes 262144 | tf_op jit(solution)/shard_map/all_to_all | solution.py:212

commit v4 on v3

--- a/solution.py
+++ b/solution.py
@@ -5,7 +5,6 @@
 from jax import lax
 from jax.experimental import pallas as pl
 from jax.experimental.pallas import tpu as pltpu
-from jax.sharding import Mesh
 from jax.sharding import PartitionSpec as P
 
 DH = 128
@@ -95,7 +94,8 @@
         copy.wait()
     for s in range(place.shape[0]):
         r = owner_here[s]
-        place[s] = lax.rem(r, columns) * rows + lax.div(r, columns)
+        x, z = lax.div(r, columns), lax.rem(r, columns)
+        place[s] = lax.rem(z + columns // 2, columns) * rows + lax.rem(x + rows // 2, rows)
 
 
 def attend(place, length, query_all, cache_kv, dense, peak_at, total_at, summed_at):
@@ -179,8 +179,14 @@
     return pl.BlockSpec((d, DH), lambda i: (0, j))
 
 
-def shards(tokens, norm_gain, w_qkv, persist_kv, memory, cache_kv, piece_owner, piece_len, w_out):
-    rows, columns = lax.axis_size("x"), lax.axis_size("z")
+def exchange_order(rows, columns):
+    return [
+        (x + rows // 2) % rows * columns + (z + columns // 2) % columns for z in range(columns) for x in range(rows)
+    ]
+
+
+def shards(rows, columns, tokens, norm_gain, w_qkv, persist_kv, memory, cache_kv, piece_owner, piece_len, w_out):
+    groups = [exchange_order(rows, columns)]
     heads = lax.axis_size("head")
     d = tokens.shape[1]
     pieces, slots = cache_kv.shape[:2]
@@ -209,7 +215,7 @@
         name="project",
     )(*held_in(pltpu.HBM, tokens, norm_gain.reshape(1, d)), w_qkv)
 
-    query_all = lax.all_to_all(query_all, ("z", "x"), 0, 0, tiled=True)
+    query_all = lax.all_to_all(query_all, "req", 0, 0, axis_index_groups=groups, tiled=True)
 
     own, recalled, cache_kv, w_out, place, piece_len = pl.pallas_call(
         functools.partial(own_part, rows, columns),
@@ -243,7 +249,7 @@
         name="attend",
     )(*held_in(pltpu.SMEM, place, piece_len), *held_in(pltpu.VMEM, query_all, cache_kv))
 
-    received = lax.all_to_all(dense, ("z", "x"), 0, 0, tiled=True)
+    received = lax.all_to_all(dense, "req", 0, 0, axis_index_groups=groups, tiled=True)
 
     partial_out = pl.pallas_call(
         merge,
@@ -259,18 +265,17 @@
 
 
 def solution(mesh):
-    mesh = Mesh(mesh.devices.reshape(4, 16, 8), ("x", "z", "head"))
-    req = ("x", "z")
     in_specs = (
-        P(req, None),
+        P("req", None),
         P(),
         P(None, "head", None),
         P("head", None, None),
-        P(req, "head", None, None),
-        P(req, None, "head", None),
-        P(req),
-        P(req),
+        P("req", "head", None, None),
+        P("req", None, "head", None),
+        P("req"),
+        P("req"),
         P("head", None, None),
     )
-    out_specs = P(req, "head")
-    return jax.shard_map(shards, mesh=mesh, in_specs=in_specs, out_specs=out_specs, check_vma=False)
+    out_specs = P("req", "head")
+    step = functools.partial(shards, 4, mesh.shape["req"] // 4)
+    return jax.shard_map(step, mesh=mesh, in_specs=in_specs, out_specs=out_specs, check_vma=False)

time: 72.9 us -> 65.4 us (0.90)
  waiting for transfers between devices: 12.2 us -> 3.51 us
  starting transfers between devices: 19.1 us -> 22.9 us
  blocking collectives: 33.7 us -> 31.1 us
    all_to_all x1, waiting for transfers between devices: 12.2 us -> 3.51 us  [shards(): lax.all_to_all(query_all, 'req', 0, 0, axis_index_groups=groups, tiled=True)]
    all_to_all x1, starting transfers between devices: 19.1 us -> 22.9 us  [shards(): lax.all_to_all(query_all, 'req', 0, 0, axis_index_groups=groups, tiled=True)]
    all_to_all x1, blocking collectives: 12.4 us -> 10.3 us  [shards(): terms = lax.all_to_all(partial_out, 'head', 0, 0, tiled=True)]
where the time goes in v4:
time: 65.4 us; the launch traced here: 65.1 us
  blocking collectives  31.1 us (48%)
  starting transfers between devices  22.9 us (35%)
  Pallas kernels  7 us (11%)
  waiting for transfers between devices  3.51 us (5%)
    all_to_all x1, starting transfers between devices, shards(): lax.all_to_all(query_all, 'req', 0, 0, axis_index_groups=groups, tiled=True)  22.9 us
    all_to_all x1, blocking collectives, shards(): lax.all_to_all(dense, 'req', 0, 0, axis_index_groups=groups, tiled=True)  20.8 us
    all_to_all x1, blocking collectives, shards(): terms = lax.all_to_all(partial_out, 'head', 0, 0, tiled=True)  10.3 us
    all_to_all x1, waiting for transfers between devices, shards(): lax.all_to_all(query_all, 'req', 0, 0, axis_index_groups=groups, tiled=True)  3.51 us
    pallas_call x1, Pallas kernels, shards(): pl.pallas_call(functools.partial(own_part, rows, columns), grid=(1,), out...  2.67 us
    pallas_call x1, Pallas kernels, shards(): pl.pallas_call(attend, out_shape=pltpu.VMEM(dense_shape, bf16), in_specs=...  2.01 us
    pallas_call x1, Pallas kernels, shards(): pl.pallas_call(project, grid=(1,), out_shape=(pltpu.VMEM(dense_shape, bf1...  1.87 us
  transfers between devices with their start and end apart: 1, of which 1 were waited for; matrix products, arithmetic and copies ran while one was open for 0% of the time, Pallas kernels for 4%

profile of v4, /device:TPU:1, one launch (start us, length us, event | category | flops | bytes accessed | tf_op | source)
XLA Modules:
  0.0 65.1 jit_solution(1536123648041868805)
XLA Ops:
  0.0 1.9 %project.1 = (bf16[64,8,128]{2,1,0:T(8,128)(2,1)}, bf16[8,128]{1,0:T(8,128)(2,1)S(1)}, bf16[5,1024]{1,0:T(8,128)(2,1)S(1)}) custom-call(bf16[5,1024]{1,0:T(8,128)(2,1)} %tokens.1, f32[1,1024]{1,0:T(1,128)} %bitcast.14, bf16[1024,384]{1,0:T(8,128)(2,1)} %bitcast.7), custom_call_target="tpu_custom_call" | custom-call | tf_op jit(solution)/shard_map/project/pallas_call | solution.py:207
  1.9 22.9 %all-to-all-start = ((bf16[64,8,128]{2,1,0:T(8,128)(2,1)}), bf16[64,8,128]{2,1,0:T(8,128)(2,1)S(1)}, u32[]{:S(2)}, u32[]{:S(2)}) async-start(bf16[64,8,128]{2,1,0:T(8,128)(2,1)} %get-tuple-element.18), calls=%async_computation | async-start | bytes 262144 | tf_op jit(solution)/shard_map/all_to_all | solution.py:218
  24.7 2.7 %own_part.1 = (f32[8,128]{1,0:T(8,128)S(1)}, f32[8,128]{1,0:T(8,128)S(1)}, bf16[8,512,256]{2,1,0:T(8,128)(2,1)S(1)}, bf16[128,1024]{1,0:T(8,128)(2,1)S(1)}, s32[8]{0:T(128)S(4)}, /*index=5*/s32[8]{0:T(128)S(4)}) custom-call(bf16[5,1024]{1,0:T(8,128)(2,1)S(1)} %get-tuple-element.14.normed, bf16[8,128]{1,0:T(8,128)(2,1)S(1)} %get-tuple-element.15.query, ...), custom_call_target="tpu_custom_call" | custom-call | tf_op jit(solution)/shard_map/own_part/pallas_call | solution.py:220
  27.4 3.5 %all-to-all-done.query_all = bf16[64,8,128]{2,1,0:T(8,128)(2,1)S(1)} async-done(((bf16[64,8,128]{2,1,0:T(8,128)(2,1)}), bf16[64,8,128]{2,1,0:T(8,128)(2,1)S(1)}, u32[]{:S(2)}, u32[]{:S(2)}) %all-to-all-start) | async-done | bytes 131104 | tf_op jit(solution)/shard_map/all_to_all | solution.py:218
  30.9 2.0 %attend.1 = bf16[64,8,128]{2,1,0:T(8,128)(2,1)S(1)} custom-call(s32[8]{0:T(128)S(4)} %get-tuple-element.16.place, s32[8]{0:T(128)S(4)} %get-tuple-element.17.length, bf16[64,8,128]{2,1,0:T(8,128)(2,1)S(1)} %all-to-all-done.query_all, bf16[8,512,256]{2,1,0:T(8,128)(2,1)S(1)} %get-tuple-element.19.cache_kv), custom_call_target="tpu_custom_call" | custom-call | tf_op jit(solution)/shard_map/attend/pallas_call | solution.py:242
  33.0 20.8 %all_to_all.15.received = bf16[64,8,128]{2,1,0:T(8,128)(2,1)S(1)} all-to-all(bf16[64,8,128]{2,1,0:T(8,128)(2,1)S(1)} %attend.1), channel_id=1, replica_groups={{320,448,64,192,328,456,72,200,336,464,80,208,344,472,88,216,352,480,96..., dimensions={0} | all-to-all | bytes 262144 | tf_op jit(solution)/shard_map/all_to_all | solution.py:252
  53.8 0.4 merge.1
  54.2 10.3 %all_to_all.16 = f32[8,8,128]{2,1,0:T(8,128)S(1)} all-to-all(f32[8,8,128]{2,1,0:T(8,128)S(1)} %merge.1), channel_id=1, replica_groups=mesh['req'=64,'head'=8] {'head'}, dimensions={0} | all-to-all | bytes 65536 | tf_op jit(solution)/shard_map/all_to_all | solution.py:263
  64.5 0.6 reduce_sum.9
Async XLA Ops:
  1.9 29.1 %all-to-all-start = ((bf16[64,8,128]{2,1,0:T(8,128)(2,1)}), bf16[64,8,128]{2,1,0:T(8,128)(2,1)S(1)}, u32[]{:S(2)}, u32[]{:S(2)}) async-start(bf16[64,8,128]{2,1,0:T(8,128)(2,1)} %get-tuple-element.18), calls=%async_computation | async-start | bytes 262144 | tf_op jit(solution)/shard_map/all_to_all | solution.py:218

commit v5 on v4

--- a/solution.py
+++ b/solution.py
@@ -11,6 +11,9 @@
 NP = 16
 Q = 5
 ROWS = 8
+PAIRS = 3
+STRIDE = 16
+PARTS = 3
 
 masked_score = -1e30
 norm_eps = 1e-06
@@ -31,14 +34,18 @@
     return lax.dot_general(a, b, (((1,), (1,)), ((), ())), preferred_element_type=f32)
 
 
+def stats_at(row, lane, offset):
+    return (lane % STRIDE == row + offset) & (lane < PARTS * STRIDE)
+
+
 def stats_row(peak, total, row, lane):
-    picked = jnp.where(lane == row, peak, jnp.where(lane == row + ROWS, total, 0.0))
+    picked = jnp.where(stats_at(row, lane, 0), peak, jnp.where(stats_at(row, lane, ROWS), total, 0.0))
     return jnp.sum(picked, axis=0, keepdims=True)
 
 
-def to_col(values, row, lane):
-    spread = jnp.broadcast_to(values, row.shape)
-    return jnp.sum(jnp.where(row == lane, spread, 0.0), axis=1, keepdims=True)
+def stats_col(block, row, lane, offset):
+    spread = jnp.broadcast_to(block[Q : Q + 1], row.shape)
+    return jnp.sum(jnp.where(stats_at(row, lane, offset), spread, 0.0), axis=1, keepdims=True)
 
 
 def packed(peak, total, summed, row, lane):
@@ -46,9 +53,19 @@
     high = stats.astype(bf16).astype(f32)
     rest = stats - high
     middle = rest.astype(bf16).astype(f32)
-    low = rest - middle
-    tail = jnp.where(row == Q, high, jnp.where(row == Q + 1, middle, low))
-    return jnp.where(row < Q, summed, tail).astype(bf16)
+    place = lane[:1]
+    tail = jnp.where(place < STRIDE, high, jnp.where(place < 2 * STRIDE, middle, rest - middle))
+    return jnp.where(row < Q, summed, tail)
+
+
+def put_block(target, index, tile):
+    for k in range(PAIRS):
+        target[index, k] = tile[2 * k : 2 * k + 2].astype(bf16)
+
+
+def get_block(source, index):
+    pairs = [source[index, k].astype(f32) for k in range(PAIRS)]
+    return jnp.concatenate(pairs + [jnp.zeros((ROWS - 2 * PAIRS, DH), f32)], axis=0)
 
 
 def project(tokens, gain, w_query, query_all, query, normed, padded):
@@ -57,9 +74,11 @@
     normed[...] = (xf * inverse * gain[...]).astype(bf16)
     padded[...] = jnp.zeros_like(padded)
     padded[0:Q, :] = dot(normed[...], w_query[...])
-    q = (padded[...] * DH ** (-0.5)).astype(bf16)
-    query[...] = q
-    query_all[...] = jnp.broadcast_to(q[None], query_all.shape)
+    q = padded[...] * DH ** (-0.5)
+    query[...] = q.astype(bf16)
+    for k in range(PAIRS):
+        pair = q[2 * k : 2 * k + 2].astype(bf16)
+        query_all[:, k] = jnp.broadcast_to(pair[None], (query_all.shape[0],) + pair.shape)
 
 
 def own_part(rows, columns, normed, query, w_key, w_value, persist_kv, memory, cache_kv, w_out, owner, length,
@@ -88,7 +107,7 @@
     summed = dot(weight_persist.astype(bf16), persist_kv[:, DH:])
     summed = summed + dot(weight_new.astype(bf16), new_kv[:, DH:])
     stats = stats_row(jnp.broadcast_to(peak, tile), jnp.broadcast_to(total, tile), row, lane)
-    own[...] = jnp.where(row < Q, summed, jnp.where(row == Q, stats, 0.0))
+    own[...] = jnp.where(row < Q, summed, jnp.where((row == Q) & (lane < STRIDE), stats, 0.0))
     recalled[...] = dot(q, memory[...])
     for copy in copies:
         copy.wait()
@@ -98,65 +117,57 @@
         place[s] = lax.rem(z + columns // 2, columns) * rows + lax.rem(x + rows // 2, rows)
 
 
-def attend(place, length, query_all, cache_kv, dense, peak_at, total_at, summed_at):
+def attend(place, length, query_all, cache_kv, dense):
     pieces, slots = cache_kv.shape[0], cache_kv.shape[1]
     tile = (ROWS, DH)
     row, lane = iota(tile, 0), iota(tile, 1)
 
-    empty = jnp.where((row == Q) & (lane < ROWS), masked_score, 0.0).astype(bf16)
-    dense[...] = jnp.broadcast_to(empty[None], dense.shape)
-    for s in range(pieces):
-        r = place[s]
-        peak_at[r] = jnp.full(tile, masked_score, f32)
-        total_at[r] = jnp.zeros(tile, f32)
-        summed_at[r] = jnp.zeros(tile, f32)
+    for k in range(PAIRS):
+        pair = (2, DH)
+        holds_peak = (iota(pair, 0) + 2 * k == Q) & (iota(pair, 1) < ROWS)
+        empty = jnp.where(holds_peak, masked_score, 0.0).astype(bf16)
+        dense[:, k] = jnp.broadcast_to(empty[None], (dense.shape[0],) + pair)
 
     slot = iota((ROWS, slots), 1)
     parts = []
     for s in range(pieces):
         valid = slot < length[s]
-        score = jnp.where(valid, dot_t(query_all[place[s]], cache_kv[s, :, :DH]), masked_score)
+        score = jnp.where(valid, dot_t(get_block(query_all, place[s]).astype(bf16), cache_kv[s, :, :DH]), masked_score)
         peak = jnp.max(score, axis=-1, keepdims=True)
         weight = jnp.where(valid, jnp.exp(score - peak), 0.0)
         total = jnp.sum(weight, axis=-1, keepdims=True)
-        parts.append((peak, total, dot(weight.astype(bf16), cache_kv[s, :, DH:])))
+        summed = dot(weight.astype(bf16), cache_kv[s, :, DH:])
+        parts.append((jnp.broadcast_to(peak, tile), jnp.broadcast_to(total, tile), summed))
 
     for s in range(pieces):
         r = place[s]
-        peak, total, summed = parts[s]
-        before = peak_at[r]
-        joint = jnp.maximum(before, peak)
-        scale_before = jnp.exp(before - joint)
-        scale = jnp.exp(peak - joint)
-        peak_at[r] = joint
-        total_at[r] = total_at[r] * scale_before + total * scale
-        summed_at[r] = summed_at[r] * scale_before + summed * scale
-    for s in range(pieces):
-        r = place[s]
-        dense[r] = packed(peak_at[r], total_at[r], summed_at[r], row, lane)
+        peaks = [jnp.where(jnp.full(tile, place[t], jnp.int32) == r, parts[t][0], 2 * masked_score) for t in range(pieces)]
+        top = functools.reduce(jnp.maximum, peaks)
+        scales = [jnp.exp(peak - top) for peak in peaks]
+        total = sum(scale * part[1] for scale, part in zip(scales, parts))
+        summed = sum(scale * part[2] for scale, part in zip(scales, parts))
+        put_block(dense, r, packed(top, total, summed, row, lane))
 
 
 def merge(received, own, recalled, w_out, partial_out):
     tile = (ROWS, DH)
     row, lane = iota(tile, 0), iota(tile, 1)
     sources = received.shape[0]
-    blocks = [own[...]] + [received[s].astype(f32) for s in range(sources)]
-    stats = [jnp.sum(jnp.where(row >= Q, block, 0.0), axis=0, keepdims=True) for block in blocks]
-    peak = stats[0]
-    for each in stats[1:]:
-        peak = jnp.maximum(peak, each)
+    blocks = [own[...]] + [get_block(received, s) for s in range(sources)]
+    peaks = [stats_col(block, row, lane, 0) for block in blocks]
+    peak = functools.reduce(jnp.maximum, peaks)
     summed = jnp.zeros(tile, f32)
     total = jnp.zeros((ROWS, 1), f32)
-    for block, each in zip(blocks, stats):
+    for block, each in zip(blocks, peaks):
         scale = jnp.exp(each - peak)
-        col = to_col(scale, row, lane)
-        total = total + col * to_col(each, row, lane - ROWS)
-        summed = summed + block * col
+        total = total + scale * stats_col(block, row, lane, ROWS)
+        summed = summed + scale * block
     attended = summed / total
     head_out = jnp.where(row < Q, attended + recalled[...], 0.0).astype(bf16)
     terms = dot(head_out, w_out[...])
     for h in range(partial_out.shape[0]):
-        partial_out[h] = terms[:, h * DH : (h + 1) * DH]
+        to = (h + partial_out.shape[0] // 2) % partial_out.shape[0]
+        partial_out[h] = terms[:, to * DH : (to + 1) * DH]
 
 
 def held_in(space, *arrays):
@@ -191,7 +202,7 @@
     d = tokens.shape[1]
     pieces, slots = cache_kv.shape[:2]
     tile = (ROWS, DH)
-    dense_shape = (rows * columns,) + tile
+    dense_shape = (rows * columns, PAIRS, 2, DH)
     params = pltpu.CompilerParams(vmem_limit_bytes=kernel_vmem)
 
     w_qkv, persist_kv, memory, cache_kv, w_out, piece_owner, piece_len = held_in(
@@ -244,7 +255,6 @@
         out_shape=pltpu.VMEM(dense_shape, bf16),
         in_specs=smem(2) + vmem(2),
         out_specs=vmem(1)[0],
-        scratch_shapes=[pltpu.VMEM(dense_shape, f32)] * 3,
         compiler_params=params,
         name="attend",
     )(*held_in(pltpu.SMEM, place, piece_len), *held_in(pltpu.VMEM, query_all, cache_kv))
@@ -260,7 +270,9 @@
         name="merge",
     )(*held_in(pltpu.VMEM, received, own, recalled, w_out))
 
-    terms = lax.all_to_all(partial_out, "head", 0, 0, tiled=True)
+    half = heads // 2
+    head_groups = [[(h + half) % heads for h in range(heads)]]
+    terms = lax.all_to_all(partial_out, "head", 0, 0, axis_index_groups=head_groups, tiled=True)
     return jnp.sum(terms, axis=0)[:Q].astype(bf16)
 
 

time: 65.4 us -> 60.9 us (0.931)
  blocking collectives: 31.1 us -> 27.7 us
  waiting for transfers between devices: 3.51 us -> 2.41 us
    all_to_all x1, blocking collectives: 20.8 us -> 18 us  [shards(): lax.all_to_all(dense, 'req', 0, 0, axis_index_groups=groups, tiled=True)]
    all_to_all x1, waiting for transfers between devices: 3.51 us -> 2.41 us  [shards(): lax.all_to_all(query_all, 'req', 0, 0, axis_index_groups=groups, tiled=True)]
where the time goes in v5:
time: 60.9 us; the launch traced here: 60.6 us
  blocking collectives  27.7 us (45%)
  starting transfers between devices  22.9 us (38%)
  Pallas kernels  7 us (11%)
  waiting for transfers between devices  2.41 us (4%)
    all_to_all x1, starting transfers between devices, shards(): lax.all_to_all(query_all, 'req', 0, 0, axis_index_groups=groups, tiled=True)  22.9 us
    all_to_all x1, blocking collectives, shards(): lax.all_to_all(dense, 'req', 0, 0, axis_index_groups=groups, tiled=True)  18 us
    all_to_all x1, blocking collectives, shards(): lax.all_to_all(partial_out, 'head', 0, 0, axis_index_groups=head_groups,...  9.68 us
    pallas_call x1, Pallas kernels, shards(): pl.pallas_call(functools.partial(own_part, rows, columns), grid=(1,), out...  2.67 us
    all_to_all x1, waiting for transfers between devices, shards(): lax.all_to_all(query_all, 'req', 0, 0, axis_index_groups=groups, tiled=True)  2.41 us
    pallas_call x1, Pallas kernels, shards(): pl.pallas_call(attend, out_shape=pltpu.VMEM(dense_shape, bf16), in_specs=...  2.04 us
    pallas_call x1, Pallas kernels, shards(): pl.pallas_call(project, grid=(1,), out_shape=(pltpu.VMEM(dense_shape, bf1...  1.9 us
  transfers between devices with their start and end apart: 1, of which 1 were waited for; matrix products, arithmetic and copies ran while one was open for 0% of the time, Pallas kernels for 4%

profile of v5, /device:TPU:1, one launch (start us, length us, event | category | flops | bytes accessed | tf_op | source)
XLA Modules:
  0.0 60.6 jit_solution(3264249574978025427)
XLA Ops:
  0.0 1.9 %project.1 = (bf16[64,3,2,128]{3,2,1,0:T(2,128)(2,1)}, bf16[8,128]{1,0:T(8,128)(2,1)S(1)}, bf16[5,1024]{1,0:T(8,128)(2,1)S(1)}) custom-call(bf16[5,1024]{1,0:T(8,128)(2,1)} %tokens.1, f32[1,1024]{1,0:T(1,128)} %bitcast.14, bf16[1024,384]{1,0:T(8,128)(2,1)} %bitcast.7), custom_call_target="tpu_custom_call" | custom-call | tf_op jit(solution)/shard_map/project/pallas_call | solution.py:218
  1.9 22.9 %all-to-all-start = ((bf16[64,3,2,128]{3,2,1,0:T(2,128)(2,1)}), bf16[64,3,2,128]{3,2,1,0:T(2,128)(2,1)S(1)}, u32[]{:S(2)}, u32[]{:S(2)}) async-start(bf16[64,3,2,128]{3,2,1,0:T(2,128)(2,1)} %get-tuple-element.18), calls=%async_computation | async-start | bytes 196608 | tf_op jit(solution)/shard_map/all_to_all | solution.py:229
  24.8 2.7 %own_part.1 = (f32[8,128]{1,0:T(8,128)S(1)}, f32[8,128]{1,0:T(8,128)S(1)}, bf16[8,512,256]{2,1,0:T(8,128)(2,1)S(1)}, bf16[128,1024]{1,0:T(8,128)(2,1)S(1)}, s32[8]{0:T(128)S(4)}, /*index=5*/s32[8]{0:T(128)S(4)}) custom-call(bf16[5,1024]{1,0:T(8,128)(2,1)S(1)} %get-tuple-element.14.normed, bf16[8,128]{1,0:T(8,128)(2,1)S(1)} %get-tuple-element.15.query, ...), custom_call_target="tpu_custom_call" | custom-call | tf_op jit(solution)/shard_map/own_part/pallas_call | solution.py:231
  27.5 2.4 %all-to-all-done.query_all = bf16[64,3,2,128]{3,2,1,0:T(2,128)(2,1)S(1)} async-done(((bf16[64,3,2,128]{3,2,1,0:T(2,128)(2,1)}), bf16[64,3,2,128]{3,2,1,0:T(2,128)(2,1)S(1)}, u32[]{:S(2)}, u32[]{:S(2)}) %all-to-all-start) | async-done | bytes 98336 | tf_op jit(solution)/shard_map/all_to_all | solution.py:229
  29.9 2.0 %attend.1 = bf16[64,3,2,128]{3,2,1,0:T(2,128)(2,1)S(1)} custom-call(s32[8]{0:T(128)S(4)} %get-tuple-element.16.place, s32[8]{0:T(128)S(4)} %get-tuple-element.17.length, bf16[64,3,2,128]{3,2,1,0:T(2,128)(2,1)S(1)} %all-to-all-done.query_all, bf16[8,512,256]{2,1,0:T(8,128)(2,1)S(1)} %get-tuple-element.19.cache_kv), custom_call_target="tpu_custom_call" | custom-call | tf_op jit(solution)/shard_map/attend/pallas_call | solution.py:253
  31.9 18.0 %all_to_all.15.received = bf16[64,3,2,128]{3,2,1,0:T(2,128)(2,1)S(1)} all-to-all(bf16[64,3,2,128]{3,2,1,0:T(2,128)(2,1)S(1)} %attend.1), channel_id=1, replica_groups={{320,448,64,192,328,456,72,200,336,464,80,208,344,472,88,216,352,480,96..., dimensions={0} | all-to-all | bytes 196608 | tf_op jit(solution)/shard_map/all_to_all | solution.py:262
  49.9 0.4 merge.1
  50.3 9.7 %all_to_all.16 = f32[8,8,128]{2,1,0:T(8,128)S(1)} all-to-all(f32[8,8,128]{2,1,0:T(8,128)S(1)} %merge.1), channel_id=1, replica_groups={{4,5,6,7,0,1,2,3},{12,13,14,15,8,9,10,11},{20,21,22,23,16,17,18,19},{28..., dimensions={0} | all-to-all | bytes 65536 | tf_op jit(solution)/shard_map/all_to_all | solution.py:275
  60.0 0.6 reduce_sum.9
Async XLA Ops:
  1.9 28.0 %all-to-all-start = ((bf16[64,3,2,128]{3,2,1,0:T(2,128)(2,1)}), bf16[64,3,2,128]{3,2,1,0:T(2,128)(2,1)S(1)}, u32[]{:S(2)}, u32[]{:S(2)}) async-start(bf16[64,3,2,128]{3,2,1,0:T(2,128)(2,1)} %get-tuple-element.18), calls=%async_computation | async-start | bytes 196608 | tf_op jit(solution)/shard_map/all_to_all | solution.py:229

commit v6 on v5

--- a/solution.py
+++ b/solution.py
@@ -129,15 +129,20 @@
         dense[:, k] = jnp.broadcast_to(empty[None], (dense.shape[0],) + pair)
 
     slot = iota((ROWS, slots), 1)
-    parts = []
+    scores = [
+        dot_t(get_block(query_all, place[s]).astype(bf16), cache_kv[s, :, :DH]) for s in range(pieces)
+    ]
+    weights, peaks, totals = [], [], []
     for s in range(pieces):
         valid = slot < length[s]
-        score = jnp.where(valid, dot_t(get_block(query_all, place[s]).astype(bf16), cache_kv[s, :, :DH]), masked_score)
+        score = jnp.where(valid, scores[s], masked_score)
         peak = jnp.max(score, axis=-1, keepdims=True)
         weight = jnp.where(valid, jnp.exp(score - peak), 0.0)
-        total = jnp.sum(weight, axis=-1, keepdims=True)
-        summed = dot(weight.astype(bf16), cache_kv[s, :, DH:])
-        parts.append((jnp.broadcast_to(peak, tile), jnp.broadcast_to(total, tile), summed))
+        weights.append(weight.astype(bf16))
+        peaks.append(jnp.broadcast_to(peak, tile))
+        totals.append(jnp.broadcast_to(jnp.sum(weight, axis=-1, keepdims=True), tile))
+    summeds = [dot(weights[s], cache_kv[s, :, DH:]) for s in range(pieces)]
+    parts = list(zip(peaks, totals, summeds))
 
     for s in range(pieces):
         r = place[s]

time: 60.9 us -> 59.5 us (0.977)
  Pallas kernels: 7 us -> 5.59 us
    pallas_call x1, Pallas kernels: 2.04 us -> 0.62 us  [shards(): pl.pallas_call(attend, out_shape=pltpu.VMEM(dense_shape, bf16), in_specs=...]
  transfers between devices with their start and end apart: 1 -> 1, of which waited for: 1 -> 1; matrix products, arithmetic and copies ran while one was open for 0% -> 0% of each run, Pallas kernels for 4% -> 5%
where the time goes in v6:
time: 59.5 us; the launch traced here: 59.2 us
  blocking collectives  27.7 us (47%)
  starting transfers between devices  22.9 us (38%)
  Pallas kernels  5.59 us (9%)
  waiting for transfers between devices  2.41 us (4%)
    all_to_all x1, starting transfers between devices, shards(): lax.all_to_all(query_all, 'req', 0, 0, axis_index_groups=groups, tiled=True)  22.9 us
    all_to_all x1, blocking collectives, shards(): lax.all_to_all(dense, 'req', 0, 0, axis_index_groups=groups, tiled=True)  18 us
    all_to_all x1, blocking collectives, shards(): lax.all_to_all(partial_out, 'head', 0, 0, axis_index_groups=head_groups,...  9.68 us
    pallas_call x1, Pallas kernels, shards(): pl.pallas_call(functools.partial(own_part, rows, columns), grid=(1,), out...  2.67 us
    all_to_all x1, waiting for transfers between devices, shards(): lax.all_to_all(query_all, 'req', 0, 0, axis_index_groups=groups, tiled=True)  2.41 us
    pallas_call x1, Pallas kernels, shards(): pl.pallas_call(project, grid=(1,), out_shape=(pltpu.VMEM(dense_shape, bf1...  1.9 us
  transfers between devices with their start and end apart: 1, of which 1 were waited for; matrix products, arithmetic and copies ran while one was open for 0% of the time, Pallas kernels for 5%

profile of v6, /device:TPU:1, one launch (start us, length us, event | category | flops | bytes accessed | tf_op | source)
XLA Modules:
  0.0 59.2 jit_solution(17638979200827851289)
XLA Ops:
  0.0 1.9 %project.1 = (bf16[64,3,2,128]{3,2,1,0:T(2,128)(2,1)}, bf16[8,128]{1,0:T(8,128)(2,1)S(1)}, bf16[5,1024]{1,0:T(8,128)(2,1)S(1)}) custom-call(bf16[5,1024]{1,0:T(8,128)(2,1)} %tokens.1, f32[1,1024]{1,0:T(1,128)} %bitcast.14, bf16[1024,384]{1,0:T(8,128)(2,1)} %bitcast.7), custom_call_target="tpu_custom_call" | custom-call | tf_op jit(solution)/shard_map/project/pallas_call | solution.py:223
  1.9 22.9 %all-to-all-start = ((bf16[64,3,2,128]{3,2,1,0:T(2,128)(2,1)}), bf16[64,3,2,128]{3,2,1,0:T(2,128)(2,1)S(1)}, u32[]{:S(2)}, u32[]{:S(2)}) async-start(bf16[64,3,2,128]{3,2,1,0:T(2,128)(2,1)} %get-tuple-element.18), calls=%async_computation | async-start | bytes 196608 | tf_op jit(solution)/shard_map/all_to_all | solution.py:234
  24.8 2.7 %own_part.1 = (f32[8,128]{1,0:T(8,128)S(1)}, f32[8,128]{1,0:T(8,128)S(1)}, bf16[8,512,256]{2,1,0:T(8,128)(2,1)S(1)}, bf16[128,1024]{1,0:T(8,128)(2,1)S(1)}, s32[8]{0:T(128)S(4)}, /*index=5*/s32[8]{0:T(128)S(4)}) custom-call(bf16[5,1024]{1,0:T(8,128)(2,1)S(1)} %get-tuple-element.14.normed, bf16[8,128]{1,0:T(8,128)(2,1)S(1)} %get-tuple-element.15.query, ...), custom_call_target="tpu_custom_call" | custom-call | tf_op jit(solution)/shard_map/own_part/pallas_call | solution.py:236
  27.5 2.4 %all-to-all-done.query_all = bf16[64,3,2,128]{3,2,1,0:T(2,128)(2,1)S(1)} async-done(((bf16[64,3,2,128]{3,2,1,0:T(2,128)(2,1)}), bf16[64,3,2,128]{3,2,1,0:T(2,128)(2,1)S(1)}, u32[]{:S(2)}, u32[]{:S(2)}) %all-to-all-start) | async-done | bytes 98336 | tf_op jit(solution)/shard_map/all_to_all | solution.py:234
  29.9 0.6 %attend.1 = bf16[64,3,2,128]{3,2,1,0:T(2,128)(2,1)S(1)} custom-call(s32[8]{0:T(128)S(4)} %get-tuple-element.16.place, s32[8]{0:T(128)S(4)} %get-tuple-element.17.length, bf16[64,3,2,128]{3,2,1,0:T(2,128)(2,1)S(1)} %all-to-all-done.query_all, bf16[8,512,256]{2,1,0:T(8,128)(2,1)S(1)} %get-tuple-element.19.cache_kv), custom_call_target="tpu_custom_call" | custom-call | tf_op jit(solution)/shard_map/attend/pallas_call | solution.py:258
  30.5 18.0 %all_to_all.15.received = bf16[64,3,2,128]{3,2,1,0:T(2,128)(2,1)S(1)} all-to-all(bf16[64,3,2,128]{3,2,1,0:T(2,128)(2,1)S(1)} %attend.1), channel_id=1, replica_groups={{320,448,64,192,328,456,72,200,336,464,80,208,344,472,88,216,352,480,96..., dimensions={0} | all-to-all | bytes 196608 | tf_op jit(solution)/shard_map/all_to_all | solution.py:267
  48.5 0.4 merge.1
  48.9 9.7 %all_to_all.16 = f32[8,8,128]{2,1,0:T(8,128)S(1)} all-to-all(f32[8,8,128]{2,1,0:T(8,128)S(1)} %merge.1), channel_id=1, replica_groups={{4,5,6,7,0,1,2,3},{12,13,14,15,8,9,10,11},{20,21,22,23,16,17,18,19},{28..., dimensions={0} | all-to-all | bytes 65536 | tf_op jit(solution)/shard_map/all_to_all | solution.py:280
  58.6 0.6 reduce_sum.9
Async XLA Ops:
  1.9 28.0 %all-to-all-start = ((bf16[64,3,2,128]{3,2,1,0:T(2,128)(2,1)}), bf16[64,3,2,128]{3,2,1,0:T(2,128)(2,1)S(1)}, u32[]{:S(2)}, u32[]{:S(2)}) async-start(bf16[64,3,2,128]{3,2,1,0:T(2,128)(2,1)} %get-tuple-element.18), calls=%async_computation | async-start | bytes 196608 | tf_op jit(solution)/shard_map/all_to_all | solution.py:234

commit v7 on v6

--- a/solution.py
+++ b/solution.py
@@ -114,7 +114,7 @@
     for s in range(place.shape[0]):
         r = owner_here[s]
         x, z = lax.div(r, columns), lax.rem(r, columns)
-        place[s] = lax.rem(z + columns // 2, columns) * rows + lax.rem(x + rows // 2, rows)
+        place[s] = lax.rem((z + columns // 2) * (columns // 2 + 1), columns) * rows + lax.rem((x + rows // 2) * (rows - 1), rows)
 
 
 def attend(place, length, query_all, cache_kv, dense):
@@ -197,7 +197,9 @@
 
 def exchange_order(rows, columns):
     return [
-        (x + rows // 2) % rows * columns + (z + columns // 2) % columns for z in range(columns) for x in range(rows)
+        (x * (rows - 1) + rows // 2) % rows * columns + (z * (columns // 2 + 1) + columns // 2) % columns
+        for z in range(columns)
+        for x in range(rows)
     ]
 
 

time: 59.5 us -> 59.3 us (level)
  no operation moved by 1% of the time
where the time goes in v7:
time: 59.3 us; the launch traced here: 59 us
  blocking collectives  27.8 us (47%)
  starting transfers between devices  22.9 us (39%)
  Pallas kernels  5.59 us (9%)
  waiting for transfers between devices  2.16 us (4%)
    all_to_all x1, starting transfers between devices, shards(): lax.all_to_all(query_all, 'req', 0, 0, axis_index_groups=groups, tiled=True)  22.9 us
    all_to_all x1, blocking collectives, shards(): lax.all_to_all(dense, 'req', 0, 0, axis_index_groups=groups, tiled=True)  17.9 us
    all_to_all x1, blocking collectives, shards(): lax.all_to_all(partial_out, 'head', 0, 0, axis_index_groups=head_groups,...  9.83 us
    pallas_call x1, Pallas kernels, shards(): pl.pallas_call(functools.partial(own_part, rows, columns), grid=(1,), out...  2.67 us
    all_to_all x1, waiting for transfers between devices, shards(): lax.all_to_all(query_all, 'req', 0, 0, axis_index_groups=groups, tiled=True)  2.16 us
    pallas_call x1, Pallas kernels, shards(): pl.pallas_call(project, grid=(1,), out_shape=(pltpu.VMEM(dense_shape, bf1...  1.9 us
  transfers between devices with their start and end apart: 1, of which 1 were waited for; matrix products, arithmetic and copies ran while one was open for 0% of the time, Pallas kernels for 5%

profile of v7, /device:TPU:1, one launch (start us, length us, event | category | flops | bytes accessed | tf_op | source)
XLA Modules:
  0.0 59.0 jit_solution(16185225568701252050)
XLA Ops:
  0.0 1.9 %project.1 = (bf16[64,3,2,128]{3,2,1,0:T(2,128)(2,1)}, bf16[8,128]{1,0:T(8,128)(2,1)S(1)}, bf16[5,1024]{1,0:T(8,128)(2,1)S(1)}) custom-call(bf16[5,1024]{1,0:T(8,128)(2,1)} %tokens.1, f32[1,1024]{1,0:T(1,128)} %bitcast.14, bf16[1024,384]{1,0:T(8,128)(2,1)} %bitcast.7), custom_call_target="tpu_custom_call" | custom-call | tf_op jit(solution)/shard_map/project/pallas_call | solution.py:225
  1.9 22.9 %all-to-all-start = ((bf16[64,3,2,128]{3,2,1,0:T(2,128)(2,1)}), bf16[64,3,2,128]{3,2,1,0:T(2,128)(2,1)S(1)}, u32[]{:S(2)}, u32[]{:S(2)}) async-start(bf16[64,3,2,128]{3,2,1,0:T(2,128)(2,1)} %get-tuple-element.18), calls=%async_computation | async-start | bytes 196608 | tf_op jit(solution)/shard_map/all_to_all | solution.py:236
  24.8 2.7 %own_part.1 = (f32[8,128]{1,0:T(8,128)S(1)}, f32[8,128]{1,0:T(8,128)S(1)}, bf16[8,512,256]{2,1,0:T(8,128)(2,1)S(1)}, bf16[128,1024]{1,0:T(8,128)(2,1)S(1)}, s32[8]{0:T(128)S(4)}, /*index=5*/s32[8]{0:T(128)S(4)}) custom-call(bf16[5,1024]{1,0:T(8,128)(2,1)S(1)} %get-tuple-element.14.normed, bf16[8,128]{1,0:T(8,128)(2,1)S(1)} %get-tuple-element.15.query, ...), custom_call_target="tpu_custom_call" | custom-call | tf_op jit(solution)/shard_map/own_part/pallas_call | solution.py:238
  27.5 2.2 %all-to-all-done.query_all = bf16[64,3,2,128]{3,2,1,0:T(2,128)(2,1)S(1)} async-done(((bf16[64,3,2,128]{3,2,1,0:T(2,128)(2,1)}), bf16[64,3,2,128]{3,2,1,0:T(2,128)(2,1)S(1)}, u32[]{:S(2)}, u32[]{:S(2)}) %all-to-all-start) | async-done | bytes 98336 | tf_op jit(solution)/shard_map/all_to_all | solution.py:236
  29.6 0.6 %attend.1 = bf16[64,3,2,128]{3,2,1,0:T(2,128)(2,1)S(1)} custom-call(s32[8]{0:T(128)S(4)} %get-tuple-element.16.place, s32[8]{0:T(128)S(4)} %get-tuple-element.17.length, bf16[64,3,2,128]{3,2,1,0:T(2,128)(2,1)S(1)} %all-to-all-done.query_all, bf16[8,512,256]{2,1,0:T(8,128)(2,1)S(1)} %get-tuple-element.19.cache_kv), custom_call_target="tpu_custom_call" | custom-call | tf_op jit(solution)/shard_map/attend/pallas_call | solution.py:260
  30.3 17.9 %all_to_all.15.received = bf16[64,3,2,128]{3,2,1,0:T(2,128)(2,1)S(1)} all-to-all(bf16[64,3,2,128]{3,2,1,0:T(2,128)(2,1)S(1)} %attend.1), channel_id=1, replica_groups={{320,192,64,448,264,136,8,392,336,208,80,464,280,152,24,408,352,224,96,..., dimensions={0} | all-to-all | bytes 196608 | tf_op jit(solution)/shard_map/all_to_all | solution.py:269
  48.2 0.4 merge.1
  48.6 9.8 %all_to_all.16 = f32[8,8,128]{2,1,0:T(8,128)S(1)} all-to-all(f32[8,8,128]{2,1,0:T(8,128)S(1)} %merge.1), channel_id=1, replica_groups={{4,5,6,7,0,1,2,3},{12,13,14,15,8,9,10,11},{20,21,22,23,16,17,18,19},{28..., dimensions={0} | all-to-all | bytes 65536 | tf_op jit(solution)/shard_map/all_to_all | solution.py:282
  58.4 0.6 reduce_sum.9
Async XLA Ops:
  1.9 27.7 %all-to-all-start = ((bf16[64,3,2,128]{3,2,1,0:T(2,128)(2,1)}), bf16[64,3,2,128]{3,2,1,0:T(2,128)(2,1)S(1)}, u32[]{:S(2)}, u32[]{:S(2)}) async-start(bf16[64,3,2,128]{3,2,1,0:T(2,128)(2,1)} %get-tuple-element.18), calls=%async_computation | async-start | bytes 196608 | tf_op jit(solution)/shard_map/all_to_all | solution.py:236
